TPU v7x, 128 devices: a whole 4x4x4 slice. The times are simulated.
128 devices in a mesh: samp: 32 (over x, y, core), var: 4 (over z).
Axes of the slice: x: 4, y: 4, z: 4, core: 2. Of those that a mesh axis runs over, the one named last changes fastest.
Arguments:
- genotypes: int32 [32768, 4096], P('samp', 'var'), may hold values from 0 to 2
- observed: int32 [32768, 4096], P('samp', 'var'), may hold values from 0 to 1, as said below
- proportions: float32 [10, 32768], P(None, 'samp'), may hold values from 0 to 1, as said below
- frequencies: float32 [10, 4096], P(None, ('samp', 'var')), may hold values from 0.02 to 0.98
Outputs:
- mixture: float32 [10, 32768], P(None, 'samp')
- alleles: float32 [10, 4096], P(None, 'var')
Inputs may be any that keep to these rules, and one draw needn't show every extreme that they name: Every sample is observed at 256 or more variants and every variant at 2048 or more samples. Each sample's 10 proportions are positive and sum to one.
All inputs are finite; a program needn't handle non-finite values.
Results may differ from a plain program's by a relative error of at most 0.0003.
Values sent between devices are 32-bit elements; how exact they have to be, the bound alone decides.
A program may use at most 128 MiB of HBM per device.

v0:
```python
import jax
import jax.numpy as jnp
from jax import lax
from jax.sharding import PartitionSpec as P

STEPS = 2


CLIP_LOW = 1e-05
NORM_EPS = 1e-10
EXACT = lax.Precision.HIGHEST


def clip_unit(values):
    return jnp.clip(values, CLIP_LOW, 1.0 - CLIP_LOW)


def tidy_mixture(mixture):
    clipped = clip_unit(mixture)
    return clipped / jnp.sum(clipped, axis=0, keepdims=True)


def step_size(first, second):
    return jnp.maximum(1.0, jnp.sqrt(first / (second + NORM_EPS)))


def allele_rule(alleles, alt_sums, ref_sums):
    weighted = alleles * alt_sums
    return clip_unit(weighted / (weighted + (1.0 - alleles) * ref_sums))


def local(genotypes, observed, proportions, frequencies):
    var_count = lax.axis_size("var")
    gathered = lax.all_gather(frequencies, ("samp", "var"), axis=1, tiled=True)
    owner_width = gathered.shape[1] // var_count
    alleles = lax.dynamic_slice_in_dim(
        gathered, lax.axis_index("var") * owner_width, owner_width, 1
    )
    seen_vals = observed.astype(jnp.float32)
    geno_vals = genotypes.astype(jnp.float32)
    alt_counts = seen_vals * geno_vals
    ref_counts = seen_vals * (2.0 - geno_vals)
    local_counts = jnp.sum(observed, axis=1).astype(jnp.float32)
    twice_observed = 2.0 * lax.psum(local_counts, "var")[None, :]

    def expectation_step(mixture, current):
        expected = lax.dot_general(
            mixture,
            current,
            (((0,), (0,)), ((), ())),
            precision=EXACT,
            preferred_element_type=jnp.float32,
        )
        ratio_alt = alt_counts / expected
        ratio_ref = ref_counts / (1.0 - expected)
        prop_terms = lax.dot_general(
            current,
            ratio_alt - ratio_ref,
            (((1,), (1,)), ((), ())),
            precision=EXACT,
            preferred_element_type=jnp.float32,
        )
        prop_terms = prop_terms + jnp.sum(ratio_ref, axis=1)[None, :]
        alt_terms = lax.dot_general(
            mixture,
            ratio_alt,
            (((1,), (0,)), ((), ())),
            precision=EXACT,
            preferred_element_type=jnp.float32,
        )
        ref_terms = lax.dot_general(
            mixture,
            ratio_ref,
            (((1,), (0,)), ((), ())),
            precision=EXACT,
            preferred_element_type=jnp.float32,
        )
        prop_sums = lax.psum(prop_terms, "var")
        next_mixture = clip_unit(mixture * prop_sums / twice_observed)
        alt_sums, ref_sums = lax.psum((alt_terms, ref_terms), "samp")
        next_alleles = allele_rule(current, alt_sums, ref_sums)
        return (next_mixture, next_alleles)

    mixture = proportions
    for repeat in range(STEPS):
        mixture_one, alleles_one = expectation_step(mixture, alleles)
        mixture_two, alleles_two = expectation_step(mixture_one, alleles_one)
        step_mix = mixture_one - mixture
        curve_mix = mixture_two - mixture_one - step_mix
        step_allele = alleles_one - alleles
        curve_allele = alleles_two - alleles_one - step_allele
        step_mix_local = jnp.sum(step_mix * step_mix)
        curve_mix_local = jnp.sum(curve_mix * curve_mix)
        step_allele_local = jnp.sum(step_allele * step_allele)
        curve_allele_local = jnp.sum(curve_allele * curve_allele)
        step_allele_sum, curve_allele_sum = lax.psum((step_allele_local, curve_allele_local), "var")
        step_mix_sum, curve_mix_sum = lax.psum((step_mix_local, curve_mix_local), "samp")
        alpha_mix = step_size(step_mix_sum, curve_mix_sum)
        alpha_allele = step_size(step_allele_sum, curve_allele_sum)
        extra_mix = tidy_mixture(
            mixture + 2.0 * alpha_mix * step_mix + alpha_mix * alpha_mix * curve_mix
        )
        extra_allele = clip_unit(
            alleles + 2.0 * alpha_allele * step_allele + alpha_allele * alpha_allele * curve_allele
        )
        mixture, alleles = expectation_step(extra_mix, extra_allele)
    return (mixture, alleles)


def solution(mesh):
    placed = (P("samp", "var"), P("samp", "var"), P(None, "samp"), P(None, ("samp", "var")))
    return jax.shard_map(
        local,
        mesh=mesh,
        in_specs=placed,
        out_specs=(P(None, "samp"), P(None, "var")),
        check_vma=False,
    )
```

profile of v0, /device:TPU:1, one launch (start us, length us, event | category | flops | bytes accessed | tf_op | source)
XLA Modules:
  0.0 984.4 jit_solution(3233084332891088129)
XLA Ops:
  7.2 64.1 %all-gather = f32[128,32,10]{1,2,0:T(8,128)S(1)} all-gather(f32[1,32,10]{1,2,0:T(8,128)} %bitcast.70), channel_id=1, replica_groups=mesh['samp'=32,'var'=4] {'samp','var'}, dimensions={0}, use_global_device_ids=true | all-gather | bytes 165120 | tf_op jit(solution)/shard_map/all_gather | solution.py:34
  71.8 5.4 copy.14
  77.2 5.4 copy.13
  82.6 12.0 %fusion.78 = (f32[1024]{0:T(1024)S(1)}, f32[1024,1024]{0,1:T(8,128)S(1)}, f32[1024,1024]{0,1:T(8,128)}, f32[1024,1024]{0,1:T(8,128)S(1)}, f32[1024,1024]{1,0:T(8,128)S(1)}) fusion(s32[1024,1024]{0,1:T(8,128)} %copy.14, s32[1024,1024]{0,1:T(8,128)} %copy.13, f32[10,1024]{1,0:T(8,128)S(1)} %copy-done.11, f32[4096,10]{0,1:T(8,128)S(1)} %reshape.15, ...), kind=kOutput, calls=%fused_computation.104 | convolution fusion | flops 134216704 | bytes 25300996 | tf_op jit(solution)/shard_map/dot_general | solution.py:47
  94.6 2.0 copy-done
  96.5 4.3 convolution_bitcast_fusion
  100.8 4.7 convolution_bitcast_fusion.1
  105.9 2.5 reduce_sum.154
  108.3 7.3 fusion.13
  115.7 13.0 %all-reduce.8 = (f32[10,1024]{1,0:T(8,128)S(1)}, f32[1024]{0:T(1024)S(1)}) all-reduce(f32[10,1024]{1,0:T(8,128)S(1)} %fusion.13, f32[1024]{0:T(1024)S(1)} %convert_element_type.11), channel_id=1, replica_groups=mesh['samp'=32,'var'=4] {'var'}, use_global_device_ids=true, to_apply=%region_1.0 | all-reduce | flops 11264 | bytes 90112 | tf_op jit(solution)/shard_map/psum | solution.py:78
  128.7 76.3 %all-reduce.22.cloned.1.call-done = (f32[10,1024]{1,0:T(8,128)}, f32[10,1024]{1,0:T(8,128)}) async-done(((f32[10,1024]{1,0:T(8,128)}, f32[10,1024]{1,0:T(8,128)}), (f32[10,1024]{1,0:T(8,128)}, f32[10,1024]{1,0:T(8,128)})) %all-reduce.22.cloned.1.call-update) | async-done | bytes 81936 | tf_op jit(solution)/shard_map/psum | solution.py:80
  205.0 1.5 multiply_reduce_fusion.5
  206.6 9.0 fusion.77
  215.6 3.5 fusion.65
  219.1 3.5 fusion.80
  222.6 2.7 fusion.16
  225.3 14.0 %psum.194 = f32[10,1024]{1,0:T(8,128)S(1)} all-reduce(f32[10,1024]{1,0:T(8,128)S(1)} %fusion.16), channel_id=1, replica_groups=mesh['samp'=32,'var'=4] {'var'}, use_global_device_ids=true, to_apply=%region_9.10 | all-reduce | flops 10240 | bytes 81920 | tf_op jit(solution)/shard_map/psum | solution.py:78
  239.9 125.1 %all-reduce.23 = (f32[10,1024]{1,0:T(8,128)S(1)}, f32[10,1024]{1,0:T(8,128)S(1)}, f32[]{:T(128)}, f32[]{:T(128)}) all-reduce(f32[10,1024]{1,0:T(8,128)S(1)} %fusion.80, f32[10,1024]{1,0:T(8,128)S(1)} %fusion.65, f32[]{:T(128)} %get-tuple-element.5, f32[]{:T(128)} %get-tuple-element.4), channel_id=1, replica_groups=mesh['samp'=32,'var'=4] {'samp'}, use_global_device_ids=true, to_apply=%region_16.17 | all-reduce | flops 20482 | bytes 163856 | tf_op jit(solution)/shard_map/psum | solution.py:80
  367.0 6.8 all-reduce.7
  375.2 9.0 fusion.73
  384.3 4.2 fusion.50
  388.4 4.2 fusion.49
  392.7 7.3 fusion.19
  400.0 12.7 %psum.200 = f32[10,1024]{1,0:T(8,128)S(1)} all-reduce(f32[10,1024]{1,0:T(8,128)S(1)} %fusion.19), channel_id=1, replica_groups=mesh['samp'=32,'var'=4] {'var'}, use_global_device_ids=true, to_apply=%region_20.21 | all-reduce | flops 10240 | bytes 81920 | tf_op jit(solution)/shard_map/psum | solution.py:78
  413.1 106.4 %all-reduce.20.cloned.1.call-done = (f32[10,1024]{1,0:T(8,128)}, f32[10,1024]{1,0:T(8,128)}) async-done(((f32[10,1024]{1,0:T(8,128)}, f32[10,1024]{1,0:T(8,128)}), (f32[10,1024]{1,0:T(8,128)}, f32[10,1024]{1,0:T(8,128)})) %all-reduce.20.cloned.1.call-update) | async-done | bytes 81936 | tf_op jit(solution)/shard_map/psum | solution.py:80
  519.5 0.9 fusion.35
  520.4 9.0 fusion.72
  529.4 4.2 fusion.60
  533.6 4.2 fusion.81
  537.8 7.3 fusion.22
  545.2 14.0 %psum.203 = f32[10,1024]{1,0:T(8,128)S(1)} all-reduce(f32[10,1024]{1,0:T(8,128)S(1)} %fusion.22), channel_id=1, replica_groups=mesh['samp'=32,'var'=4] {'var'}, use_global_device_ids=true, to_apply=%region_24.25 | all-reduce | flops 10240 | bytes 81920 | tf_op jit(solution)/shard_map/psum | solution.py:78
  559.6 102.1 %all-reduce.18.cloned.1.call-done = (f32[10,1024]{1,0:T(8,128)}, f32[10,1024]{1,0:T(8,128)}) async-done(((f32[10,1024]{1,0:T(8,128)}, f32[10,1024]{1,0:T(8,128)}), (f32[10,1024]{1,0:T(8,128)}, f32[10,1024]{1,0:T(8,128)})) %all-reduce.18.cloned.1.call-update) | async-done | bytes 81936 | tf_op jit(solution)/shard_map/psum | solution.py:80
  661.8 0.9 fusion.36
  662.7 9.0 fusion.71
  671.7 3.5 fusion.57
  675.2 3.5 fusion.82
  678.8 2.7 fusion.25
  681.5 14.0 %psum.207 = f32[10,1024]{1,0:T(8,128)S(1)} all-reduce(f32[10,1024]{1,0:T(8,128)S(1)} %fusion.25), channel_id=1, replica_groups=mesh['samp'=32,'var'=4] {'var'}, use_global_device_ids=true, to_apply=%region_30.31 | all-reduce | flops 10240 | bytes 81920 | tf_op jit(solution)/shard_map/psum | solution.py:78
  696.1 125.1 %all-reduce.24 = (f32[10,1024]{1,0:T(8,128)S(1)}, f32[10,1024]{1,0:T(8,128)S(1)}, f32[]{:T(128)}, f32[]{:T(128)}) all-reduce(f32[10,1024]{1,0:T(8,128)S(1)} %fusion.82, f32[10,1024]{1,0:T(8,128)S(1)} %fusion.57, f32[]{:T(128)} %get-tuple-element.3, f32[]{:T(128)} %get-tuple-element.2), channel_id=1, replica_groups=mesh['samp'=32,'var'=4] {'samp'}, use_global_device_ids=true, to_apply=%region_37.38 | all-reduce | flops 20482 | bytes 163856 | tf_op jit(solution)/shard_map/psum | solution.py:80
  823.7 6.8 all-reduce.6
  832.0 9.0 fusion.68
  841.0 4.2 fusion.53
  845.2 4.2 fusion.52
  849.4 7.3 fusion.28
  856.7 12.7 %psum.213 = f32[10,1024]{1,0:T(8,128)S(1)} all-reduce(f32[10,1024]{1,0:T(8,128)S(1)} %fusion.28), channel_id=1, replica_groups=mesh['samp'=32,'var'=4] {'var'}, use_global_device_ids=true, to_apply=%region_41.42 | all-reduce | flops 10240 | bytes 81920 | tf_op jit(solution)/shard_map/psum | solution.py:78
  869.5 0.7 divide_clamp_fusion
  870.2 106.0 %all-reduce.16.cloned.1.call-done = (f32[10,1024]{1,0:T(8,128)}, f32[10,1024]{1,0:T(8,128)}) async-done(((f32[10,1024]{1,0:T(8,128)}, f32[10,1024]{1,0:T(8,128)}), (f32[10,1024]{1,0:T(8,128)}, f32[10,1024]{1,0:T(8,128)})) %all-reduce.16.cloned.1.call-update) | async-done | bytes 81936 | tf_op jit(solution)/shard_map/psum | solution.py:80
  976.2 1.5 fusion.40
  (52 shorter events, 5.2 us)
Async XLA Ops:
  7.2 197.9 %all-reduce.22.cloned.1.call-start = ((), (), s32[]{:S(2)}) async-start(), calls=%async_computation.3 | async-start | bytes 262144 | tf_op jit(solution)/shard_map/psum | solution.py:80
  77.2 5.4 copy-start.11
  94.6 2.0 copy-start
  94.6 6.2 copy-start.4
  94.6 6.2 copy-start.10
  105.5 414.0 %all-reduce.20.cloned.1.call-start = ((), (), s32[]{:S(2)}) async-start(), calls=%async_computation.2 | async-start | bytes 262144 | tf_op jit(solution)/shard_map/psum | solution.py:80
  206.6 9.0 copy-start.5
  375.2 9.1 copy-start.6
  384.2 4.2 copy-start.13
  384.3 4.2 copy-start.2
  412.8 249.0 %all-reduce.18.cloned.1.call-start = ((), (), s32[]{:S(2)}) async-start(), calls=%async_computation.1 | async-start | bytes 262144 | tf_op jit(solution)/shard_map/psum | solution.py:80
  520.4 9.1 copy-start.7
  529.4 4.2 copy-start.14
  529.4 4.2 copy-start.3
  559.1 417.0 %all-reduce.16.cloned.1.call-start = ((), (), s32[]{:S(2)}) async-start(), calls=%async_computation | async-start | bytes 262144 | tf_op jit(solution)/shard_map/psum | solution.py:80
  662.7 9.0 copy-start.8
  832.0 9.1 copy-start.9
  841.0 4.2 copy-start.12
  841.0 4.2 copy-start.1
Sparse Core Ops, SparseCore 0:
  105.6 99.3 all-reduce.21
  412.9 106.5 all-reduce.19
  559.3 102.4 all-reduce.17
  869.6 106.4 all-reduce.15
where the time goes:
time: 994 us; the launch traced here: 984 us
  blocking collectives  408 us (41%)
  waiting for transfers between devices  391 us (39%)
  matrix products  140 us (14%)
  between operations  19.6 us (2%)
  local copies, waits for them, and re-layouts  13.3 us (1%)
  other arithmetic  11.3 us (1%)
    psum x4, waiting for transfers between devices, expectation_step(): alt_sums, ref_sums = lax.psum((alt_terms, ref_terms), 'samp')  391 us
    psum x2, blocking collectives, expectation_step(): alt_sums, ref_sums = lax.psum((alt_terms, ref_terms), 'samp')  250 us
    psum x6, blocking collectives, expectation_step(): prop_sums = lax.psum(prop_terms, 'var')  80.3 us
    all_gather x1, blocking collectives, local(): gathered = lax.all_gather(frequencies, ('samp', 'var'), axis=1, tiled=True)  64.1 us
    dot_general x6, matrix products, expectation_step(): lax.dot_general(mixture, current, (((0,), (0,)), ((), ())), precision=EXA...  57.1 us
    dot_general x6, matrix products, expectation_step(): lax.dot_general(current, ratio_alt - ratio_ref, (((1,), (1,)), ((), ())),...  34.7 us
    dot_general x6, matrix products, expectation_step(): lax.dot_general(mixture, ratio_alt, (((1,), (0,)), ((), ())), precision=E...  24.2 us
    dot_general x6, matrix products, expectation_step(): lax.dot_general(mixture, ratio_ref, (((1,), (0,)), ((), ())), precision=E...  24 us
  transfers between devices with their start and end apart: 4, of which 4 were waited for; matrix products, arithmetic and copies ran while one was open for 1% of the time, Pallas kernels for 0%

commit v1 on v0

v1 whole, which is shorter than its diff:
```python
import functools

import jax
import jax.numpy as jnp
from jax import lax
from jax.experimental import pallas as pl
from jax.experimental.pallas import tpu as pltpu
from jax.sharding import PartitionSpec as P

STEPS = 2
CLIP_LOW = 1e-05
NORM_EPS = 1e-10
MESH = pl.DeviceIdType.MESH

K = 10
ROWS = 16
NS = 32
NV = 4
SAMP = 1024
VARS = 1024
LANES = 128
TILES = VARS // LANES
PIECES = 24
RB = 256
CB = 256
CHUNK = 128
CHUNKS = SAMP // CHUNK

F32 = jnp.float32
BF16 = jnp.bfloat16


def clip_unit(values):
    return jnp.clip(values, CLIP_LOW, 1.0 - CLIP_LOW)


def split3(values):
    high = values.astype(BF16).astype(F32)
    rest = values - high
    mid = rest.astype(BF16).astype(F32)
    low = (rest - mid).astype(BF16).astype(F32)
    return high, mid, low


def split2(values):
    high = values.astype(BF16)
    low = (values - high.astype(F32)).astype(BF16)
    return high, low


def dot(a, b):
    return lax.dot_general(
        a, b, (((1,), (0,)), ((), ())), preferred_element_type=F32
    )


def owner_of(piece):
    return lax.rem(piece, 16) * 2 + piece // 16


def kernel(
    geno_hbm,
    seen_hbm,
    props_ref,
    freqs_ref,
    mix_ref,
    allele_ref,
    geno_buf,
    seen_buf,
    alt_cnt,
    ref_cnt,
    count_acc,
    prop_acc,
    q_now,
    q_start,
    q_one,
    p_now,
    p_start,
    p_one,
    q_cols,
    p_rows,
    q_rows,
    p_cols,
    f_send,
    f_recv,
    tile_all,
    rs_send,
    rs_recv,
    ag_all,
    z_all,
    sq_q,
    sq_p,
    load_sem,
    f_sems,
    t_sems,
    rs_sems,
    ag_sems,
    z_send,
    z_recv,
    sq_sems,
    sp_sems,
):
    s = lax.axis_index("samp")
    v = lax.axis_index("var")
    my_piece = lax.rem(s, 2) * 16 + s // 2
    is_owner = my_piece < PIECES
    my_q = my_piece // TILES
    my_t = lax.rem(my_piece, TILES)
    home = s // TILES
    tile_here = home == v
    t_first = v * TILES

    def remote(src, dst, send_sem, recv_sem, where):
        return pltpu.make_async_remote_copy(
            src_ref=src,
            dst_ref=dst,
            send_sem=send_sem,
            recv_sem=recv_sem,
            device_id=where,
            device_id_type=MESH,
        )

    def wait_bytes(ref, sem):
        pltpu.make_async_copy(ref, ref, sem).wait()

    def load(chunk):
        rows = pl.ds(chunk * CHUNK, CHUNK)
        return (
            pltpu.make_async_copy(geno_hbm.at[rows], geno_buf.at[rows], load_sem.at[0, chunk]),
            pltpu.make_async_copy(seen_hbm.at[rows], seen_buf.at[rows], load_sem.at[1, chunk]),
        )

    for chunk in range(CHUNKS):
        for copy in load(chunk):
            copy.start()

    barrier = pltpu.get_barrier_semaphore()

    def greet_samp(d, carry):
        pl.semaphore_signal(barrier, inc=1, device_id=(lax.rem(s + d, NS), v), device_id_type=MESH)
        return carry

    def greet_var(d, carry):
        pl.semaphore_signal(barrier, inc=1, device_id=(s, lax.rem(v + d, NV)), device_id_type=MESH)
        return carry

    lax.fori_loop(1, NV, greet_var, 0)
    lax.fori_loop(1, NS, greet_samp, 0)

    row_ids = lax.broadcasted_iota(jnp.int32, (ROWS, 1), 0)
    row_mask = row_ids < K

    block = jnp.concatenate([freqs_ref[...], jnp.zeros((ROWS - K, 32), F32)], axis=0)
    block = jnp.concatenate([block, block, block, block], axis=1)
    lane_group = lax.broadcasted_iota(jnp.int32, (ROWS, LANES), 1) // 32
    block = jnp.where(lane_group == v, block, 0.0)
    f_send[...] = block
    q_now[...] = jnp.concatenate([props_ref[...], jnp.zeros((ROWS - K, SAMP), F32)], axis=0)

    pl.semaphore_wait(barrier, NS - 1 + NV - 1)

    @pl.when(jnp.logical_not(tile_here))
    def _():
        remote(f_send, f_recv.at[v], f_sems.at[0], f_sems.at[1], (s, home)).start()

    lane_ids = lax.broadcasted_iota(jnp.int32, (VARS, LANES), 1)
    count_w = jnp.where(lane_ids == 3 * ROWS + K, 2.0, 0.0).astype(BF16)

    def convert(chunk):
        for copy in load(chunk):
            copy.wait()
        rows = pl.ds(chunk * CHUNK, CHUNK)
        seen = seen_buf[rows, :].astype(F32)
        alt = seen * geno_buf[rows, :].astype(F32)
        alt_cnt[rows, :] = alt
        ref_cnt[rows, :] = 2.0 * seen - alt
        count_acc[rows, :] = dot(seen.astype(BF16), count_w)

    for chunk in range(CHUNKS // 2):
        convert(chunk)

    @pl.when(tile_here)
    def _():
        wait_bytes(f_recv.at[pl.ds(0, NV - 1)], f_sems.at[1])
        f_recv[v] = block
        tile = f_recv[0] + f_recv[1] + f_recv[2] + f_recv[3]
        tile_all[lax.rem(s, TILES)] = tile

        def send_tile(d, carry):
            slot = tile_all.at[lax.rem(s, TILES)]
            remote(slot, slot, t_sems.at[0], t_sems.at[1], (lax.rem(s + d, NS), v)).start()
            return carry

        lax.fori_loop(1, NS, send_tile, 0)

    for chunk in range(CHUNKS // 2, CHUNKS):
        convert(chunk)

    @pl.when(tile_here)
    def _():
        wait_bytes(tile_all.at[pl.ds(0, TILES - 1)], t_sems.at[1])

    @pl.when(jnp.logical_not(tile_here))
    def _():
        wait_bytes(tile_all, t_sems.at[1])
        remote(f_send, f_recv.at[v], f_sems.at[0], f_sems.at[1], (s, home)).wait_send()

    @pl.when(tile_here)
    def _():
        slot = tile_all.at[0]

        def drain(d, carry):
            wait_bytes(slot, t_sems.at[0])
            return carry

        lax.fori_loop(1, NS, drain, 0)

    for t in range(TILES):
        p_now[t] = tile_all[t]

    def full_p(ref):
        return jnp.concatenate([ref[t] for t in range(TILES)], axis=1)

    def em_step(step, carry):
        phase = lax.rem(step, 3)
        parity = lax.rem(step, 2)
        q = q_now[...]
        p = full_p(p_now)
        qh, qm, ql = split3(q)
        ph, pm, pL = split3(p)
        pad = jnp.zeros((2 * ROWS, SAMP), F32)
        pad5 = jnp.zeros((5 * ROWS, SAMP), F32)
        q_cols[...] = jnp.concatenate([qh, qh, qm, qm, qh, ql, pad], axis=0).T.astype(BF16)
        p_rows[...] = jnp.concatenate([ph, pm, ph, pm, pL, ph, pad], axis=0).astype(BF16)
        q_rows[...] = jnp.concatenate([qh, qm, ql], axis=0).astype(BF16)
        p_cols[...] = jnp.concatenate([ph, pm, pL, pad5], axis=0).T.astype(BF16)

        for cb in range(VARS // CB):
            cols = pl.ds(cb * CB, CB)
            p_part = p_rows[:, cols]
            p_weights = p_cols[cols, :]

            def row_block(rb, sums):
                alt_sum, ref_sum = sums
                rows = pl.ds(pl.multiple_of(rb * RB, RB), RB)
                expected = dot(q_cols[rows, :], p_part)
                other = 1.0 - expected
                inverse = 1.0 / (expected * other)
                ratio_alt = alt_cnt[rows, cols] * (other * inverse)
                ratio_ref = ref_cnt[rows, cols] * (expected * inverse)
                alt_high, alt_low = split2(ratio_alt)
                ref_high, ref_low = split2(ratio_ref)
                diff_high, diff_low = split2(ratio_alt - ratio_ref)
                q_part = q_rows[:, rows]
                alt_sum = alt_sum + (dot(q_part, alt_high) + dot(q_part, alt_low))
                ref_sum = ref_sum + (dot(q_part, ref_high) + dot(q_part, ref_low))
                before = count_acc[rows, :] if cb == 0 else prop_acc[rows, :]
                prop_acc[rows, :] = before + (dot(diff_high, p_weights) + dot(diff_low, p_weights))
                return alt_sum, ref_sum

            zero = jnp.zeros((3 * ROWS, CB), F32)
            alt3, ref3 = zero, zero
            for rb in range(SAMP // RB):
                alt3, ref3 = row_block(rb, (alt3, ref3))
            alt = alt3[:ROWS] + alt3[ROWS : 2 * ROWS] + alt3[2 * ROWS :]
            ref = ref3[:ROWS] + ref3[ROWS : 2 * ROWS] + ref3[2 * ROWS :]
            for t in range(cb * CB // LANES, (cb + 1) * CB // LANES):
                lane = t * LANES - cb * CB
                for part in range(3):
                    piece = part * TILES + t
                    target = (piece % 16) * 2 + piece // 16
                    rs_send[piece] = jnp.concatenate(
                        [
                            alt[4 * part : 4 * part + 4, lane : lane + LANES],
                            ref[4 * part : 4 * part + 4, lane : lane + LANES],
                        ],
                        axis=0,
                    )

                    @pl.when(s != target)
                    def _():
                        remote(
                            rs_send.at[piece],
                            rs_recv.at[s],
                            rs_sems.at[0],
                            rs_sems.at[1],
                            (target, v),
                        ).start()

        turned = prop_acc[...].T
        z_all[parity, v] = (
            turned[:ROWS]
            + turned[ROWS : 2 * ROWS]
            + turned[2 * ROWS : 3 * ROWS]
            + turned[3 * ROWS : 4 * ROWS]
        )

        def send_z(d, carry):
            slot = z_all.at[parity, v]
            remote(slot, slot, z_send.at[0], z_recv.at[parity], (s, lax.rem(v + d, NV))).start()
            return carry

        lax.fori_loop(1, NV, send_z, 0)

        wait_bytes(z_all.at[parity, pl.ds(0, NV - 1)], z_recv.at[parity])
        total = z_all[parity, 0] + z_all[parity, 1] + z_all[parity, 2] + z_all[parity, 3]
        twice = total[K : K + 1, :]
        inner = jnp.sum(q * total, axis=0, keepdims=True)
        q_next = jnp.where(row_mask, clip_unit(q * (1.0 + (total - inner) / twice)), 0.0)

        @pl.when(phase == 1)
        def _():
            step_mix = q_one[...] - q_start[...]
            curve_mix = q_next - q_one[...] - step_mix
            row = [jnp.sum(a * a, axis=0, keepdims=True) for a in (step_mix, curve_mix)]
            row = jnp.concatenate(row, axis=0)
            part = row[:, :LANES]
            for t in range(1, TILES):
                part = part + row[:, t * LANES : (t + 1) * LANES]
            sq_q[s] = part

            def send_sq(d, carry):
                slot = sq_q.at[s]
                remote(slot, slot, sq_sems.at[0], sq_sems.at[1], (lax.rem(s + d, NS), v)).start()
                return carry

            lax.fori_loop(1, NS, send_sq, 0)

        @pl.when(is_owner)
        def _():
            wait_bytes(rs_recv.at[pl.ds(0, NS - 1)], rs_sems.at[1])
            rs_recv[s] = rs_send[my_piece]
            sums = [rs_recv[i] for i in range(NS)]
            while len(sums) > 1:
                sums = [sums[i] + sums[i + 1] for i in range(0, len(sums), 2)]
            alt_sum, ref_sum = sums[0][:4], sums[0][4:]
            tile = p_now[my_t]
            old = jnp.where(my_q == 0, tile[:4], jnp.where(my_q == 1, tile[4:8], tile[8:12]))
            weighted = old * alt_sum
            new = clip_unit(weighted / (weighted + (1.0 - old) * ref_sum))
            piece_row = 4 * my_q + lax.broadcasted_iota(jnp.int32, (4, LANES), 0)
            ag_all[my_piece] = jnp.where(piece_row < K, new, 0.0)

            def send_ag(d, carry):
                slot = ag_all.at[my_piece]
                remote(slot, slot, ag_sems.at[0], ag_sems.at[1], (lax.rem(s + d, NS), v)).start()
                return carry

            lax.fori_loop(1, NS, send_ag, 0)
            wait_bytes(ag_all.at[pl.ds(0, PIECES - 1)], ag_sems.at[1])

        @pl.when(jnp.logical_not(is_owner))
        def _():
            wait_bytes(ag_all, ag_sems.at[1])

        zeros4 = jnp.zeros((4, LANES), F32)
        p_next = [
            jnp.concatenate([ag_all[t], ag_all[TILES + t], ag_all[2 * TILES + t], zeros4], axis=0)
            for t in range(TILES)
        ]

        @pl.when(phase == 0)
        def _():
            q_start[...] = q
            q_one[...] = q_next
            q_now[...] = q_next
            for t in range(TILES):
                p_start[t] = p_now[t]
                p_one[t] = p_next[t]
                p_now[t] = p_next[t]

        @pl.when(phase == 2)
        def _():
            q_now[...] = q_next
            for t in range(TILES):
                p_now[t] = p_next[t]

        @pl.when(phase == 1)
        def _():
            part_r = jnp.zeros((ROWS, LANES), F32)
            part_v = jnp.zeros((ROWS, LANES), F32)
            for t in range(TILES):
                r = p_one[t] - p_start[t]
                c = p_next[t] - p_one[t] - r
                part_r = part_r + r * r
                part_v = part_v + c * c
            sq_p[v] = jnp.concatenate(
                [jnp.sum(part_r, axis=0, keepdims=True), jnp.sum(part_v, axis=0, keepdims=True)],
                axis=0,
            )

            def send_sp(d, carry):
                slot = sq_p.at[v]
                remote(slot, slot, sp_sems.at[0], sp_sems.at[1], (s, lax.rem(v + d, NV))).start()
                return carry

            lax.fori_loop(1, NV, send_sp, 0)

            def alpha_of(sums):
                first = jnp.sum(sums[0:1], axis=1, keepdims=True)
                second = jnp.sum(sums[1:2], axis=1, keepdims=True)
                return jnp.maximum(1.0, jnp.sqrt(first / (second + NORM_EPS)))

            wait_bytes(sq_q.at[pl.ds(0, NS - 1)], sq_sems.at[1])
            sums = [sq_q[i] for i in range(NS)]
            while len(sums) > 1:
                sums = [sums[i] + sums[i + 1] for i in range(0, len(sums), 2)]
            alpha = alpha_of(sums[0])
            base = q_start[...]
            step_mix = q_one[...] - base
            curve_mix = q_next - q_one[...] - step_mix
            extra = clip_unit(base + 2.0 * alpha * step_mix + alpha * alpha * curve_mix)
            extra = jnp.where(row_mask, extra, 0.0)
            q_now[...] = extra / jnp.sum(extra, axis=0, keepdims=True)

            wait_bytes(sq_p.at[pl.ds(0, NV - 1)], sp_sems.at[1])
            alpha_p = alpha_of(sq_p[0] + sq_p[1] + sq_p[2] + sq_p[3])
            for t in range(TILES):
                base_p = p_start[t]
                r = p_one[t] - base_p
                c = p_next[t] - p_one[t] - r
                extra_p = clip_unit(base_p + 2.0 * alpha_p * r + alpha_p * alpha_p * c)
                p_now[t] = jnp.where(row_mask, extra_p, 0.0)

            wait_bytes(sq_q.at[pl.ds(0, NS - 1)], sq_sems.at[0])
            wait_bytes(sq_p.at[pl.ds(0, NV - 1)], sp_sems.at[0])

        wait_bytes(z_all.at[parity, pl.ds(0, NV - 1)], z_send.at[0])
        wait_bytes(rs_send.at[pl.ds(0, PIECES - 1)], rs_sems.at[0])

        @pl.when(is_owner)
        def _():
            wait_bytes(ag_all, ag_sems.at[0])
            wait_bytes(ag_all.at[pl.ds(0, NS - 1 - PIECES)], ag_sems.at[0])

        @pl.when(jnp.logical_not(is_owner))
        def _():
            wait_bytes(rs_send.at[0], rs_sems.at[0])

        return carry

    lax.fori_loop(0, 3 * STEPS, em_step, 0)
    mix_ref[...] = q_now[:K, :]
    for t in range(TILES):
        allele_ref[:, t * LANES : (t + 1) * LANES] = p_now[t][:K]


def local(genotypes, observed, proportions, frequencies):
    vmem = pl.BlockSpec(memory_space=pltpu.VMEM)
    hbm = pl.BlockSpec(memory_space=pl.ANY)
    dma = pltpu.SemaphoreType.DMA
    return pl.pallas_call(
        kernel,
        name="em",
        out_shape=(
            jax.ShapeDtypeStruct((K, SAMP), F32),
            jax.ShapeDtypeStruct((K, VARS), F32),
        ),
        in_specs=[hbm, hbm, vmem, vmem],
        out_specs=(vmem, vmem),
        scratch_shapes=[
            pltpu.VMEM((SAMP, VARS), jnp.int32),
            pltpu.VMEM((SAMP, VARS), jnp.int32),
            pltpu.VMEM((SAMP, VARS), F32),
            pltpu.VMEM((SAMP, VARS), F32),
            pltpu.VMEM((SAMP, LANES), F32),
            pltpu.VMEM((SAMP, LANES), F32),
            pltpu.VMEM((ROWS, SAMP), F32),
            pltpu.VMEM((ROWS, SAMP), F32),
            pltpu.VMEM((ROWS, SAMP), F32),
            pltpu.VMEM((TILES, ROWS, LANES), F32),
            pltpu.VMEM((TILES, ROWS, LANES), F32),
            pltpu.VMEM((TILES, ROWS, LANES), F32),
            pltpu.VMEM((SAMP, LANES), BF16),
            pltpu.VMEM((LANES, VARS), BF16),
            pltpu.VMEM((3 * ROWS, SAMP), BF16),
            pltpu.VMEM((VARS, LANES), BF16),
            pltpu.VMEM((ROWS, LANES), F32),
            pltpu.VMEM((NV, ROWS, LANES), F32),
            pltpu.VMEM((TILES, ROWS, LANES), F32),
            pltpu.VMEM((PIECES, 8, LANES), F32),
            pltpu.VMEM((NS, 8, LANES), F32),
            pltpu.VMEM((PIECES, 4, LANES), F32),
            pltpu.VMEM((2, NV, ROWS, SAMP), F32),
            pltpu.VMEM((NS, 2, LANES), F32),
            pltpu.VMEM((NV, 2, LANES), F32),
            dma((2, CHUNKS)),
            dma((2,)),
            dma((2,)),
            dma((2,)),
            dma((2,)),
            dma((1,)),
            dma((2,)),
            dma((2,)),
            dma((2,)),
        ],
        compiler_params=pltpu.CompilerParams(
            collective_id=0, has_side_effects=True, vmem_limit_bytes=48 << 20
        ),
    )(genotypes, observed, proportions, frequencies)


def solution(mesh):
    placed = (P("samp", "var"), P("samp", "var"), P(None, "samp"), P(None, ("samp", "var")))
    return jax.shard_map(
        local,
        mesh=mesh,
        in_specs=placed,
        out_specs=(P(None, "samp"), P(None, "var")),
        check_vma=False,
    )
```

time: 994 us -> 137 us (0.14)
  blocking collectives: 408 us -> 0 us
  waiting for transfers between devices: 391 us -> 0 us
  matrix products: 140 us -> 0 us
  Pallas kernels: 0 us -> 131 us
  between operations: 19.6 us -> 0.65 us
  other arithmetic: 11.3 us -> 0 us
    psum x4 -> x0, waiting for transfers between devices: 391 us -> none  [expectation_step(): alt_sums, ref_sums = lax.psum((alt_terms, ref_terms), 'samp')]
    psum x10 -> x0, blocking collectives: 344 us -> none  [the longest x2 250 us: expectation_step(): alt_sums, ref_sums = lax.psum((alt_terms, ref_terms), 'samp')]
    dot_general x24 -> x0, matrix products: 140 us -> none  [the longest x6 57.1 us: expectation_step(): lax.dot_general(mixture, current, (((0,), (0,)), ((), ())), precision=EXA...]
    pallas_call x0 -> x1, Pallas kernels: none -> 131 us  [local(): pl.pallas_call(kernel, name='em', out_shape=(jax.ShapeDtypeStruct((K, SAM...]
    all_gather x1 -> x0, blocking collectives: 64.1 us -> none  [local(): gathered = lax.all_gather(frequencies, ('samp', 'var'), axis=1, tiled=True)]
  transfers between devices with their start and end apart: 4 -> 0, of which waited for: 4 -> 0; matrix products, arithmetic and copies ran while one was open for 1% -> 0% of each run, Pallas kernels for 0% -> 0%
where the time goes in v1:
time: 137 us; the launch traced here: 136 us
  Pallas kernels  131 us (96%)
  local copies, waits for them, and re-layouts  4.98 us (4%)
    pallas_call x1, Pallas kernels, local(): pl.pallas_call(kernel, name='em', out_shape=(jax.ShapeDtypeStruct((K, SAM...  131 us
    unnamed x8, local copies, waits for them, and re-layouts  4.98 us

profile of v1, /device:TPU:1, one launch (start us, length us, event | category | flops | bytes accessed | tf_op | source)
XLA Modules:
  0.0 136.5 jit_solution(4124736806033439019)
XLA Ops:
  0.6 0.0 copy-start
  0.6 2.2 %copy-done = s32[1024,1024]{1,0:T(8,128)S(1)} copy-done((s32[1024,1024]{1,0:T(8,128)S(1)}, s32[1024,1024]{1,0:T(8,128)}, u32[]{:S(2)}) %copy-start) | copy-done | bytes 4194328
  2.8 0.0 copy-start.1
  2.8 0.8 copy-done.1
  3.7 0.0 copy-start.2
  3.7 0.7 copy-done.2
  4.4 130.8 %em.1 = (f32[10,1024]{1,0:T(8,128)S(1)}, f32[10,1024]{1,0:T(8,128)S(1)}) custom-call(s32[1024,1024]{1,0:T(8,128)S(1)} %copy-done, s32[1024,1024]{1,0:T(8,128)} %seen_hbm.1, f32[10,1024]{1,0:T(8,128)S(1)} %copy-done.1, f32[10,32]{1,0:T(8,128)S(1)} %copy-done.2), custom_call_target="tpu_custom_call" | custom-call | tf_op jit(solution)/shard_map/em/pallas_call | solution.py:452
  135.2 0.6 copy.8
  135.8 0.6 copy.9
Async XLA Ops:
  0.6 2.2 %copy-start = (s32[1024,1024]{1,0:T(8,128)S(1)}, s32[1024,1024]{1,0:T(8,128)}, u32[]{:S(2)}) copy-start(s32[1024,1024]{1,0:T(8,128)} %geno_hbm.1) | copy-start | bytes 12582916
  2.8 0.8 copy-start.1
  3.7 0.7 copy-start.2

commit v2 on v1

--- a/solution.py
+++ b/solution.py
@@ -1,5 +1,3 @@
-import functools
-
 import jax
 import jax.numpy as jnp
 from jax import lax
@@ -23,6 +21,7 @@
 PIECES = 24
 RB = 256
 CB = 256
+BLOCKS = VARS // CB
 CHUNK = 128
 CHUNKS = SAMP // CHUNK
 
@@ -52,10 +51,6 @@
     return lax.dot_general(
         a, b, (((1,), (0,)), ((), ())), preferred_element_type=F32
     )
-
-
-def owner_of(piece):
-    return lax.rem(piece, 16) * 2 + piece // 16
 
 
 def kernel(
@@ -81,9 +76,11 @@
     p_rows,
     q_rows,
     p_cols,
+    w_buf,
+    props_buf,
+    freqs_buf,
     f_send,
     f_recv,
-    tile_all,
     rs_send,
     rs_recv,
     ag_all,
@@ -91,8 +88,8 @@
     sq_q,
     sq_p,
     load_sem,
+    small_sem,
     f_sems,
-    t_sems,
     rs_sems,
     ag_sems,
     z_send,
@@ -107,8 +104,6 @@
     my_q = my_piece // TILES
     my_t = lax.rem(my_piece, TILES)
     home = s // TILES
-    tile_here = home == v
-    t_first = v * TILES
 
     def remote(src, dst, send_sem, recv_sem, where):
         return pltpu.make_async_remote_copy(
@@ -130,38 +125,82 @@
             pltpu.make_async_copy(seen_hbm.at[rows], seen_buf.at[rows], load_sem.at[1, chunk]),
         )
 
+    small = (
+        pltpu.make_async_copy(freqs_ref, freqs_buf, small_sem.at[0]),
+        pltpu.make_async_copy(props_ref, props_buf, small_sem.at[1]),
+    )
+    for copy in small:
+        copy.start()
     for chunk in range(CHUNKS):
         for copy in load(chunk):
             copy.start()
 
     barrier = pltpu.get_barrier_semaphore()
 
+    def greet(where):
+        pl.semaphore_signal(barrier, inc=1, device_id=where, device_id_type=MESH)
+
     def greet_samp(d, carry):
-        pl.semaphore_signal(barrier, inc=1, device_id=(lax.rem(s + d, NS), v), device_id_type=MESH)
+        greet((lax.rem(s + d, NS), v))
         return carry
 
     def greet_var(d, carry):
-        pl.semaphore_signal(barrier, inc=1, device_id=(s, lax.rem(v + d, NV)), device_id_type=MESH)
+        greet((s, lax.rem(v + d, NV)))
         return carry
 
+    def greet_source(i, carry):
+        far_s = v * TILES + i // NV
+        far_v = lax.rem(i, NV)
+
+        @pl.when(jnp.logical_or(far_s != s, far_v != v))
+        def _():
+            greet((far_s, far_v))
+
+        return carry
+
+    lax.fori_loop(0, NS, greet_source, 0)
     lax.fori_loop(1, NV, greet_var, 0)
     lax.fori_loop(1, NS, greet_samp, 0)
 
     row_ids = lax.broadcasted_iota(jnp.int32, (ROWS, 1), 0)
     row_mask = row_ids < K
 
-    block = jnp.concatenate([freqs_ref[...], jnp.zeros((ROWS - K, 32), F32)], axis=0)
-    block = jnp.concatenate([block, block, block, block], axis=1)
-    lane_group = lax.broadcasted_iota(jnp.int32, (ROWS, LANES), 1) // 32
-    block = jnp.where(lane_group == v, block, 0.0)
-    f_send[...] = block
-    q_now[...] = jnp.concatenate([props_ref[...], jnp.zeros((ROWS - K, SAMP), F32)], axis=0)
-
-    pl.semaphore_wait(barrier, NS - 1 + NV - 1)
-
-    @pl.when(jnp.logical_not(tile_here))
+    small[0].wait()
+    block = freqs_buf[...]
+    tail = jnp.concatenate([block[8:K], jnp.zeros((ROWS - K, 32), F32)], axis=0)
+    f_send[...] = jnp.concatenate([block[:8], tail, jnp.zeros((8, 64), F32)], axis=1)
+
+    @pl.when(home == v)
     def _():
-        remote(f_send, f_recv.at[v], f_sems.at[0], f_sems.at[1], (s, home)).start()
+        pl.semaphore_wait(barrier, NS - 1 + NV - 1 + NS - 1)
+
+    @pl.when(home != v)
+    def _():
+        pl.semaphore_wait(barrier, NS - 1 + NV - 1 + NS)
+
+    my_slot = NV * lax.rem(s, TILES) + v
+
+    def send_block(d, carry):
+        far_s = lax.rem(s + NS // 2 + d, NS)
+
+        @pl.when(jnp.logical_or(far_s != s, home != v))
+        def _():
+            remote(f_send, f_recv.at[my_slot], f_sems.at[0], f_sems.at[1], (far_s, home)).start()
+
+        return carry
+
+    lax.fori_loop(0, NS, send_block, 0)
+
+    small[1].wait()
+    q_now[...] = jnp.concatenate([props_buf[...], jnp.zeros((ROWS - K, SAMP), F32)], axis=0)
+
+    def prep_q(q):
+        qh, qm, ql = split3(q)
+        pad = jnp.zeros((2 * ROWS, SAMP), F32)
+        q_cols[...] = jnp.concatenate([qh, qh, qm, qm, qh, ql, pad], axis=0).T.astype(BF16)
+        q_rows[...] = jnp.concatenate([qh, qm, ql], axis=0).astype(BF16)
+
+    prep_q(q_now[...])
 
     lane_ids = lax.broadcasted_iota(jnp.int32, (VARS, LANES), 1)
     count_w = jnp.where(lane_ids == 3 * ROWS + K, 2.0, 0.0).astype(BF16)
@@ -176,47 +215,38 @@
         ref_cnt[rows, :] = 2.0 * seen - alt
         count_acc[rows, :] = dot(seen.astype(BF16), count_w)
 
-    for chunk in range(CHUNKS // 2):
+    for chunk in range(CHUNKS):
         convert(chunk)
 
-    @pl.when(tile_here)
+    @pl.when(home == v)
     def _():
-        wait_bytes(f_recv.at[pl.ds(0, NV - 1)], f_sems.at[1])
-        f_recv[v] = block
-        tile = f_recv[0] + f_recv[1] + f_recv[2] + f_recv[3]
-        tile_all[lax.rem(s, TILES)] = tile
-
-        def send_tile(d, carry):
-            slot = tile_all.at[lax.rem(s, TILES)]
-            remote(slot, slot, t_sems.at[0], t_sems.at[1], (lax.rem(s + d, NS), v)).start()
-            return carry
-
-        lax.fori_loop(1, NS, send_tile, 0)
-
-    for chunk in range(CHUNKS // 2, CHUNKS):
-        convert(chunk)
-
-    @pl.when(tile_here)
+        wait_bytes(f_recv.at[pl.ds(0, NS - 1)], f_sems.at[1])
+        f_recv[my_slot] = f_send[...]
+
+    @pl.when(home != v)
     def _():
-        wait_bytes(tile_all.at[pl.ds(0, TILES - 1)], t_sems.at[1])
-
-    @pl.when(jnp.logical_not(tile_here))
+        wait_bytes(f_recv, f_sems.at[1])
+
+    lane_group = lax.broadcasted_iota(jnp.int32, (8, LANES), 1) // 32
+    for t in range(TILES):
+        halves = []
+        for half in range(2):
+            rows8 = jnp.zeros((8, LANES), F32)
+            for m in range(NV):
+                shift = (32 * (m - half)) % LANES
+                got = f_recv[NV * t + m]
+                got = pltpu.roll(got, shift, 1) if shift else got
+                rows8 = jnp.where(lane_group == m, got, rows8)
+            halves.append(rows8)
+        p_now[t] = jnp.concatenate(halves, axis=0)
+
+    @pl.when(home == v)
     def _():
-        wait_bytes(tile_all, t_sems.at[1])
-        remote(f_send, f_recv.at[v], f_sems.at[0], f_sems.at[1], (s, home)).wait_send()
-
-    @pl.when(tile_here)
+        wait_bytes(f_recv.at[pl.ds(0, NS - 1)], f_sems.at[0])
+
+    @pl.when(home != v)
     def _():
-        slot = tile_all.at[0]
-
-        def drain(d, carry):
-            wait_bytes(slot, t_sems.at[0])
-            return carry
-
-        lax.fori_loop(1, NS, drain, 0)
-
-    for t in range(TILES):
-        p_now[t] = tile_all[t]
+        wait_bytes(f_recv, f_sems.at[0])
 
     def full_p(ref):
         return jnp.concatenate([ref[t] for t in range(TILES)], axis=1)
@@ -224,46 +254,42 @@
     def em_step(step, carry):
         phase = lax.rem(step, 3)
         parity = lax.rem(step, 2)
-        q = q_now[...]
         p = full_p(p_now)
-        qh, qm, ql = split3(q)
         ph, pm, pL = split3(p)
-        pad = jnp.zeros((2 * ROWS, SAMP), F32)
-        pad5 = jnp.zeros((5 * ROWS, SAMP), F32)
-        q_cols[...] = jnp.concatenate([qh, qh, qm, qm, qh, ql, pad], axis=0).T.astype(BF16)
+        pad = jnp.zeros((2 * ROWS, VARS), F32)
+        pad5 = jnp.zeros((5 * ROWS, VARS), F32)
         p_rows[...] = jnp.concatenate([ph, pm, ph, pm, pL, ph, pad], axis=0).astype(BF16)
-        q_rows[...] = jnp.concatenate([qh, qm, ql], axis=0).astype(BF16)
-        p_cols[...] = jnp.concatenate([ph, pm, pL, pad5], axis=0).T.astype(BF16)
-
-        for cb in range(VARS // CB):
+        turned_p = jnp.concatenate([ph, pm, pL, pad5], axis=0).T
+        for cb in range(BLOCKS):
+            pos = turned_p[cb * CB : (cb + 1) * CB].astype(BF16)
+            neg = -pos
+            for kind in range(4):
+                p_cols[cb, kind * CB : (kind + 1) * CB, :] = pos if kind < 2 else neg
+
+        def stage_a(cb, rb, slot):
             cols = pl.ds(cb * CB, CB)
-            p_part = p_rows[:, cols]
-            p_weights = p_cols[cols, :]
-
-            def row_block(rb, sums):
-                alt_sum, ref_sum = sums
-                rows = pl.ds(pl.multiple_of(rb * RB, RB), RB)
-                expected = dot(q_cols[rows, :], p_part)
-                other = 1.0 - expected
-                inverse = 1.0 / (expected * other)
-                ratio_alt = alt_cnt[rows, cols] * (other * inverse)
-                ratio_ref = ref_cnt[rows, cols] * (expected * inverse)
-                alt_high, alt_low = split2(ratio_alt)
-                ref_high, ref_low = split2(ratio_ref)
-                diff_high, diff_low = split2(ratio_alt - ratio_ref)
-                q_part = q_rows[:, rows]
-                alt_sum = alt_sum + (dot(q_part, alt_high) + dot(q_part, alt_low))
-                ref_sum = ref_sum + (dot(q_part, ref_high) + dot(q_part, ref_low))
-                before = count_acc[rows, :] if cb == 0 else prop_acc[rows, :]
-                prop_acc[rows, :] = before + (dot(diff_high, p_weights) + dot(diff_low, p_weights))
-                return alt_sum, ref_sum
-
-            zero = jnp.zeros((3 * ROWS, CB), F32)
-            alt3, ref3 = zero, zero
-            for rb in range(SAMP // RB):
-                alt3, ref3 = row_block(rb, (alt3, ref3))
-            alt = alt3[:ROWS] + alt3[ROWS : 2 * ROWS] + alt3[2 * ROWS :]
-            ref = ref3[:ROWS] + ref3[ROWS : 2 * ROWS] + ref3[2 * ROWS :]
+            rows = pl.ds(rb * RB, RB)
+            expected = dot(q_cols[rows, :], p_rows[:, cols])
+            other = 1.0 - expected
+            inverse = 1.0 / (expected * other)
+            alt_high, alt_low = split2(alt_cnt[rows, cols] * (other * inverse))
+            ref_high, ref_low = split2(ref_cnt[rows, cols] * (expected * inverse))
+            for kind, part in enumerate((alt_high, alt_low, ref_high, ref_low)):
+                w_buf[slot, :, kind * CB : (kind + 1) * CB] = part
+
+        def stage_b(cb, rb, slot, sums):
+            rows = pl.ds(rb * RB, RB)
+            terms = w_buf[slot]
+            part = dot(q_rows[:, rows], terms)
+            sums = part if sums is None else sums + part
+            before = count_acc[rows, :] if cb == 0 else prop_acc[rows, :]
+            prop_acc[rows, :] = before + dot(terms, p_cols[cb])
+            return sums
+
+        def send_pieces(cb, sums):
+            folded = sums[:ROWS] + sums[ROWS : 2 * ROWS] + sums[2 * ROWS :]
+            alt = folded[:, :CB] + folded[:, CB : 2 * CB]
+            ref = folded[:, 2 * CB : 3 * CB] + folded[:, 3 * CB :]
             for t in range(cb * CB // LANES, (cb + 1) * CB // LANES):
                 lane = t * LANES - cb * CB
                 for part in range(3):
@@ -287,6 +313,17 @@
                             (target, v),
                         ).start()
 
+        units = [(cb, rb) for cb in range(BLOCKS) for rb in range(SAMP // RB)]
+        sums = None
+        stage_a(*units[0], 0)
+        for n, (cb, rb) in enumerate(units):
+            if n + 1 < len(units):
+                stage_a(*units[n + 1], (n + 1) % 2)
+            sums = stage_b(cb, rb, n % 2, sums)
+            if rb == SAMP // RB - 1:
+                send_pieces(cb, sums)
+                sums = None
+
         turned = prop_acc[...].T
         z_all[parity, v] = (
             turned[:ROWS]
@@ -301,30 +338,6 @@
             return carry
 
         lax.fori_loop(1, NV, send_z, 0)
-
-        wait_bytes(z_all.at[parity, pl.ds(0, NV - 1)], z_recv.at[parity])
-        total = z_all[parity, 0] + z_all[parity, 1] + z_all[parity, 2] + z_all[parity, 3]
-        twice = total[K : K + 1, :]
-        inner = jnp.sum(q * total, axis=0, keepdims=True)
-        q_next = jnp.where(row_mask, clip_unit(q * (1.0 + (total - inner) / twice)), 0.0)
-
-        @pl.when(phase == 1)
-        def _():
-            step_mix = q_one[...] - q_start[...]
-            curve_mix = q_next - q_one[...] - step_mix
-            row = [jnp.sum(a * a, axis=0, keepdims=True) for a in (step_mix, curve_mix)]
-            row = jnp.concatenate(row, axis=0)
-            part = row[:, :LANES]
-            for t in range(1, TILES):
-                part = part + row[:, t * LANES : (t + 1) * LANES]
-            sq_q[s] = part
-
-            def send_sq(d, carry):
-                slot = sq_q.at[s]
-                remote(slot, slot, sq_sems.at[0], sq_sems.at[1], (lax.rem(s + d, NS), v)).start()
-                return carry
-
-            lax.fori_loop(1, NS, send_sq, 0)
 
         @pl.when(is_owner)
         def _():
@@ -347,6 +360,38 @@
                 return carry
 
             lax.fori_loop(1, NS, send_ag, 0)
+
+        wait_bytes(z_all.at[parity, pl.ds(0, NV - 1)], z_recv.at[parity])
+        q = q_now[...]
+        total = z_all[parity, 0] + z_all[parity, 1] + z_all[parity, 2] + z_all[parity, 3]
+        twice = total[K : K + 1, :]
+        inner = jnp.sum(q * total, axis=0, keepdims=True)
+        q_next = jnp.where(row_mask, clip_unit(q * (1.0 + (total - inner) / twice)), 0.0)
+
+        @pl.when(phase == 1)
+        def _():
+            step_mix = q_one[...] - q_start[...]
+            curve_mix = q_next - q_one[...] - step_mix
+            row = [jnp.sum(a * a, axis=0, keepdims=True) for a in (step_mix, curve_mix)]
+            row = jnp.concatenate(row, axis=0)
+            part = row[:, :LANES]
+            for t in range(1, TILES):
+                part = part + row[:, t * LANES : (t + 1) * LANES]
+            sq_q[s] = part
+
+            def send_sq(d, carry):
+                slot = sq_q.at[s]
+                remote(slot, slot, sq_sems.at[0], sq_sems.at[1], (lax.rem(s + d, NS), v)).start()
+                return carry
+
+            lax.fori_loop(1, NS, send_sq, 0)
+
+        @pl.when(phase != 1)
+        def _():
+            prep_q(q_next)
+
+        @pl.when(is_owner)
+        def _():
             wait_bytes(ag_all.at[pl.ds(0, PIECES - 1)], ag_sems.at[1])
 
         @pl.when(jnp.logical_not(is_owner))
@@ -411,7 +456,9 @@
             curve_mix = q_next - q_one[...] - step_mix
             extra = clip_unit(base + 2.0 * alpha * step_mix + alpha * alpha * curve_mix)
             extra = jnp.where(row_mask, extra, 0.0)
-            q_now[...] = extra / jnp.sum(extra, axis=0, keepdims=True)
+            extra = extra / jnp.sum(extra, axis=0, keepdims=True)
+            q_now[...] = extra
+            prep_q(extra)
 
             wait_bytes(sq_p.at[pl.ds(0, NV - 1)], sp_sems.at[1])
             alpha_p = alpha_of(sq_p[0] + sq_p[1] + sq_p[2] + sq_p[3])
@@ -456,7 +503,7 @@
             jax.ShapeDtypeStruct((K, SAMP), F32),
             jax.ShapeDtypeStruct((K, VARS), F32),
         ),
-        in_specs=[hbm, hbm, vmem, vmem],
+        in_specs=[hbm, hbm, hbm, hbm],
         out_specs=(vmem, vmem),
         scratch_shapes=[
             pltpu.VMEM((SAMP, VARS), jnp.int32),
@@ -474,10 +521,12 @@
             pltpu.VMEM((SAMP, LANES), BF16),
             pltpu.VMEM((LANES, VARS), BF16),
             pltpu.VMEM((3 * ROWS, SAMP), BF16),
-            pltpu.VMEM((VARS, LANES), BF16),
-            pltpu.VMEM((ROWS, LANES), F32),
-            pltpu.VMEM((NV, ROWS, LANES), F32),
-            pltpu.VMEM((TILES, ROWS, LANES), F32),
+            pltpu.VMEM((BLOCKS, 4 * CB, LANES), BF16),
+            pltpu.VMEM((2, RB, 4 * CB), BF16),
+            pltpu.VMEM((K, SAMP), F32),
+            pltpu.VMEM((K, 32), F32),
+            pltpu.VMEM((8, LANES), F32),
+            pltpu.VMEM((NS, 8, LANES), F32),
             pltpu.VMEM((PIECES, 8, LANES), F32),
             pltpu.VMEM((NS, 8, LANES), F32),
             pltpu.VMEM((PIECES, 4, LANES), F32),
@@ -495,7 +544,7 @@
             dma((2,)),
         ],
         compiler_params=pltpu.CompilerParams(
-            collective_id=0, has_side_effects=True, vmem_limit_bytes=48 << 20
+            collective_id=0, has_side_effects=True, vmem_limit_bytes=60 * 1024 * 1024
         ),
     )(genotypes, observed, proportions, frequencies)
 

time: 137 us -> 115 us (0.84)
  Pallas kernels: 131 us -> 111 us
  local copies, waits for them, and re-layouts: 4.98 us -> 2.95 us
    pallas_call x1, Pallas kernels: 131 us -> 111 us  [local(): pl.pallas_call(kernel, name='em', out_shape=(jax.ShapeDtypeStruct((K, SAM...]
    unnamed x8 -> x2, local copies, waits for them, and re-layouts: 4.98 us -> 2.95 us
where the time goes in v2:
time: 115 us
  Pallas kernels  111 us (97%)
  local copies, waits for them, and re-layouts  2.95 us (3%)
    pallas_call x1, Pallas kernels, local(): pl.pallas_call(kernel, name='em', out_shape=(jax.ShapeDtypeStruct((K, SAM...  111 us
    unnamed x2, local copies, waits for them, and re-layouts  2.95 us

profile of v2, /device:TPU:1, one launch (start us, length us, event | category | flops | bytes accessed | tf_op | source)
XLA Modules:
  0.0 114.7 jit_solution(71313170935392718)
XLA Ops:
  0.6 111.1 %em.1 = (f32[10,1024]{1,0:T(8,128)}, f32[10,1024]{1,0:T(8,128)}) custom-call(s32[1024,1024]{1,0:T(8,128)} %geno_hbm.1, s32[1024,1024]{1,0:T(8,128)} %seen_hbm.1, f32[10,1024]{1,0:T(8,128)} %props_ref.1, f32[10,32]{1,0:T(8,128)} %freqs_ref.1), custom_call_target="tpu_custom_call" | custom-call | tf_op jit(solution)/shard_map/em/pallas_call | solution.py:499
  111.7 1.5 %copy.8 = f32[10,1024]{1,0:T(8,128)} copy(f32[10,1024]{1,0:T(8,128)} %get-tuple-element.4) | data formatting | bytes 81920
  113.2 1.5 %copy.9 = f32[10,1024]{1,0:T(8,128)} copy(f32[10,1024]{1,0:T(8,128)} %get-tuple-element.5) | data formatting | bytes 81920

commit v3 on v2

--- a/solution.py
+++ b/solution.py
@@ -22,6 +22,7 @@
 RB = 256
 CB = 256
 BLOCKS = VARS // CB
+GROUP = CB // LANES
 CHUNK = 128
 CHUNKS = SAMP // CHUNK
 
@@ -50,6 +51,12 @@
 def dot(a, b):
     return lax.dot_general(
         a, b, (((1,), (0,)), ((), ())), preferred_element_type=F32
+    )
+
+
+def dot_t(a, b):
+    return lax.dot_general(
+        a, b, (((1,), (1,)), ((), ())), preferred_element_type=F32
     )
 
 
@@ -68,14 +75,12 @@
     prop_acc,
     q_now,
     q_start,
-    q_one,
     p_now,
     p_start,
-    p_one,
     q_cols,
     p_rows,
     q_rows,
-    p_cols,
+    p_three,
     w_buf,
     props_buf,
     freqs_buf,
@@ -91,7 +96,8 @@
     small_sem,
     f_sems,
     rs_sems,
-    ag_sems,
+    ag_send,
+    ag_recv,
     z_send,
     z_recv,
     sq_sems,
@@ -202,8 +208,8 @@
 
     prep_q(q_now[...])
 
-    lane_ids = lax.broadcasted_iota(jnp.int32, (VARS, LANES), 1)
-    count_w = jnp.where(lane_ids == 3 * ROWS + K, 2.0, 0.0).astype(BF16)
+    count_rows = lax.broadcasted_iota(jnp.int32, (ROWS, VARS), 0)
+    count_w = jnp.where(count_rows == K, 2.0, 0.0).astype(BF16)
 
     def convert(chunk):
         for copy in load(chunk):
@@ -213,7 +219,7 @@
         alt = seen * geno_buf[rows, :].astype(F32)
         alt_cnt[rows, :] = alt
         ref_cnt[rows, :] = 2.0 * seen - alt
-        count_acc[rows, :] = dot(seen.astype(BF16), count_w)
+        count_acc[:, rows] = dot_t(count_w, seen.astype(BF16))
 
     for chunk in range(CHUNKS):
         convert(chunk)
@@ -248,23 +254,48 @@
     def _():
         wait_bytes(f_recv, f_sems.at[0])
 
-    def full_p(ref):
-        return jnp.concatenate([ref[t] for t in range(TILES)], axis=1)
+    def wait_alleles(cb):
+        mine = jnp.logical_and(is_owner, my_t // GROUP == cb)
+
+        @pl.when(mine)
+        def _():
+            wait_bytes(ag_all.at[pl.ds(0, 3 * GROUP - 1)], ag_recv.at[cb])
+
+        @pl.when(jnp.logical_not(mine))
+        def _():
+            wait_bytes(ag_all.at[pl.ds(0, 3 * GROUP)], ag_recv.at[cb])
+
+    def wait_alleles_sent():
+        @pl.when(is_owner)
+        def _():
+            wait_bytes(ag_all, ag_send.at[0])
+            wait_bytes(ag_all.at[pl.ds(0, NS - 1 - PIECES)], ag_send.at[0])
+
+    def tile_of(t):
+        return jnp.concatenate(
+            [ag_all[t], ag_all[TILES + t], ag_all[2 * TILES + t], jnp.zeros((4, LANES), F32)],
+            axis=0,
+        )
 
     def em_step(step, carry):
         phase = lax.rem(step, 3)
         parity = lax.rem(step, 2)
-        p = full_p(p_now)
-        ph, pm, pL = split3(p)
-        pad = jnp.zeros((2 * ROWS, VARS), F32)
-        pad5 = jnp.zeros((5 * ROWS, VARS), F32)
-        p_rows[...] = jnp.concatenate([ph, pm, ph, pm, pL, ph, pad], axis=0).astype(BF16)
-        turned_p = jnp.concatenate([ph, pm, pL, pad5], axis=0).T
-        for cb in range(BLOCKS):
-            pos = turned_p[cb * CB : (cb + 1) * CB].astype(BF16)
-            neg = -pos
-            for kind in range(4):
-                p_cols[cb, kind * CB : (kind + 1) * CB, :] = pos if kind < 2 else neg
+        follows = jnp.logical_or(phase == 1, jnp.logical_and(phase == 0, step > 0))
+
+        def prep_p(cb):
+            @pl.when(follows)
+            def _():
+                wait_alleles(cb)
+                for t in range(cb * GROUP, (cb + 1) * GROUP):
+                    p_start[t] = p_now[t]
+                    p_now[t] = tile_of(t)
+
+            p = jnp.concatenate([p_now[t] for t in range(cb * GROUP, (cb + 1) * GROUP)], axis=1)
+            ph, pm, pL = split3(p)
+            pad = jnp.zeros((2 * ROWS, CB), F32)
+            cols = pl.ds(cb * CB, CB)
+            p_rows[:, cols] = jnp.concatenate([ph, pm, ph, pm, pL, ph, pad], axis=0).astype(BF16)
+            p_three[...] = jnp.concatenate([ph, pm, pL], axis=0).astype(BF16)
 
         def stage_a(cb, rb, slot):
             cols = pl.ds(cb * CB, CB)
@@ -275,21 +306,24 @@
             alt_high, alt_low = split2(alt_cnt[rows, cols] * (other * inverse))
             ref_high, ref_low = split2(ref_cnt[rows, cols] * (expected * inverse))
             for kind, part in enumerate((alt_high, alt_low, ref_high, ref_low)):
-                w_buf[slot, :, kind * CB : (kind + 1) * CB] = part
+                w_buf[slot, kind] = part
 
         def stage_b(cb, rb, slot, sums):
             rows = pl.ds(rb * RB, RB)
-            terms = w_buf[slot]
-            part = dot(q_rows[:, rows], terms)
-            sums = part if sums is None else sums + part
-            before = count_acc[rows, :] if cb == 0 else prop_acc[rows, :]
-            prop_acc[rows, :] = before + dot(terms, p_cols[cb])
-            return sums
+            q_part = q_rows[:, rows]
+            p_part = p_three[...]
+            sides = []
+            props = []
+            for side in range(2):
+                high, low = w_buf[slot, 2 * side], w_buf[slot, 2 * side + 1]
+                sides.append(dot(q_part, high) + dot(q_part, low))
+                props.append(dot_t(p_part, high) + dot_t(p_part, low))
+            prop = props[0] - props[1]
+            prop_acc[:, rows] = prop if cb == 0 else prop_acc[:, rows] + prop
+            return sides if sums is None else [sums[i] + sides[i] for i in range(2)]
 
         def send_pieces(cb, sums):
-            folded = sums[:ROWS] + sums[ROWS : 2 * ROWS] + sums[2 * ROWS :]
-            alt = folded[:, :CB] + folded[:, CB : 2 * CB]
-            ref = folded[:, 2 * CB : 3 * CB] + folded[:, 3 * CB :]
+            alt, ref = [a[:ROWS] + a[ROWS : 2 * ROWS] + a[2 * ROWS :] for a in sums]
             for t in range(cb * CB // LANES, (cb + 1) * CB // LANES):
                 lane = t * LANES - cb * CB
                 for part in range(3):
@@ -313,23 +347,18 @@
                             (target, v),
                         ).start()
 
-        units = [(cb, rb) for cb in range(BLOCKS) for rb in range(SAMP // RB)]
-        sums = None
-        stage_a(*units[0], 0)
-        for n, (cb, rb) in enumerate(units):
-            if n + 1 < len(units):
-                stage_a(*units[n + 1], (n + 1) % 2)
-            sums = stage_b(cb, rb, n % 2, sums)
-            if rb == SAMP // RB - 1:
-                send_pieces(cb, sums)
-                sums = None
-
-        turned = prop_acc[...].T
-        z_all[parity, v] = (
-            turned[:ROWS]
-            + turned[ROWS : 2 * ROWS]
-            + turned[2 * ROWS : 3 * ROWS]
-            + turned[3 * ROWS : 4 * ROWS]
+        for cb in range(BLOCKS):
+            prep_p(cb)
+            sums = None
+            stage_a(cb, 0, 0)
+            for rb in range(SAMP // RB):
+                if rb + 1 < SAMP // RB:
+                    stage_a(cb, rb + 1, (rb + 1) % 2)
+                sums = stage_b(cb, rb, rb % 2, sums)
+            send_pieces(cb, sums)
+
+        z_all[parity, v] = count_acc[...] + (
+            prop_acc[:ROWS, :] + prop_acc[ROWS : 2 * ROWS, :] + prop_acc[2 * ROWS :, :]
         )
 
         def send_z(d, carry):
@@ -352,11 +381,18 @@
             weighted = old * alt_sum
             new = clip_unit(weighted / (weighted + (1.0 - old) * ref_sum))
             piece_row = 4 * my_q + lax.broadcasted_iota(jnp.int32, (4, LANES), 0)
+
+            @pl.when(step > 0)
+            def _():
+                wait_alleles_sent()
+
             ag_all[my_piece] = jnp.where(piece_row < K, new, 0.0)
 
             def send_ag(d, carry):
                 slot = ag_all.at[my_piece]
-                remote(slot, slot, ag_sems.at[0], ag_sems.at[1], (lax.rem(s + d, NS), v)).start()
+                remote(
+                    slot, slot, ag_send.at[0], ag_recv.at[my_t // GROUP], (lax.rem(s + d, NS), v)
+                ).start()
                 return carry
 
             lax.fori_loop(1, NS, send_ag, 0)
@@ -370,8 +406,8 @@
 
         @pl.when(phase == 1)
         def _():
-            step_mix = q_one[...] - q_start[...]
-            curve_mix = q_next - q_one[...] - step_mix
+            step_mix = q - q_start[...]
+            curve_mix = q_next - q - step_mix
             row = [jnp.sum(a * a, axis=0, keepdims=True) for a in (step_mix, curve_mix)]
             row = jnp.concatenate(row, axis=0)
             part = row[:, :LANES]
@@ -388,45 +424,20 @@
 
         @pl.when(phase != 1)
         def _():
+            q_start[...] = q
+            q_now[...] = q_next
             prep_q(q_next)
 
-        @pl.when(is_owner)
-        def _():
-            wait_bytes(ag_all.at[pl.ds(0, PIECES - 1)], ag_sems.at[1])
-
-        @pl.when(jnp.logical_not(is_owner))
-        def _():
-            wait_bytes(ag_all, ag_sems.at[1])
-
-        zeros4 = jnp.zeros((4, LANES), F32)
-        p_next = [
-            jnp.concatenate([ag_all[t], ag_all[TILES + t], ag_all[2 * TILES + t], zeros4], axis=0)
-            for t in range(TILES)
-        ]
-
-        @pl.when(phase == 0)
-        def _():
-            q_start[...] = q
-            q_one[...] = q_next
-            q_now[...] = q_next
-            for t in range(TILES):
-                p_start[t] = p_now[t]
-                p_one[t] = p_next[t]
-                p_now[t] = p_next[t]
-
-        @pl.when(phase == 2)
-        def _():
-            q_now[...] = q_next
-            for t in range(TILES):
-                p_now[t] = p_next[t]
-
         @pl.when(phase == 1)
         def _():
+            for cb in range(BLOCKS):
+                wait_alleles(cb)
+            p_next = [tile_of(t) for t in range(TILES)]
             part_r = jnp.zeros((ROWS, LANES), F32)
             part_v = jnp.zeros((ROWS, LANES), F32)
             for t in range(TILES):
-                r = p_one[t] - p_start[t]
-                c = p_next[t] - p_one[t] - r
+                r = p_now[t] - p_start[t]
+                c = p_next[t] - p_now[t] - r
                 part_r = part_r + r * r
                 part_v = part_v + c * c
             sq_p[v] = jnp.concatenate(
@@ -452,8 +463,8 @@
                 sums = [sums[i] + sums[i + 1] for i in range(0, len(sums), 2)]
             alpha = alpha_of(sums[0])
             base = q_start[...]
-            step_mix = q_one[...] - base
-            curve_mix = q_next - q_one[...] - step_mix
+            step_mix = q - base
+            curve_mix = q_next - q - step_mix
             extra = clip_unit(base + 2.0 * alpha * step_mix + alpha * alpha * curve_mix)
             extra = jnp.where(row_mask, extra, 0.0)
             extra = extra / jnp.sum(extra, axis=0, keepdims=True)
@@ -464,8 +475,8 @@
             alpha_p = alpha_of(sq_p[0] + sq_p[1] + sq_p[2] + sq_p[3])
             for t in range(TILES):
                 base_p = p_start[t]
-                r = p_one[t] - base_p
-                c = p_next[t] - p_one[t] - r
+                r = p_now[t] - base_p
+                c = p_next[t] - p_now[t] - r
                 extra_p = clip_unit(base_p + 2.0 * alpha_p * r + alpha_p * alpha_p * c)
                 p_now[t] = jnp.where(row_mask, extra_p, 0.0)
 
@@ -475,11 +486,6 @@
         wait_bytes(z_all.at[parity, pl.ds(0, NV - 1)], z_send.at[0])
         wait_bytes(rs_send.at[pl.ds(0, PIECES - 1)], rs_sems.at[0])
 
-        @pl.when(is_owner)
-        def _():
-            wait_bytes(ag_all, ag_sems.at[0])
-            wait_bytes(ag_all.at[pl.ds(0, NS - 1 - PIECES)], ag_sems.at[0])
-
         @pl.when(jnp.logical_not(is_owner))
         def _():
             wait_bytes(rs_send.at[0], rs_sems.at[0])
@@ -488,15 +494,23 @@
 
     lax.fori_loop(0, 3 * STEPS, em_step, 0)
     mix_ref[...] = q_now[:K, :]
+    for cb in range(BLOCKS):
+        wait_alleles(cb)
     for t in range(TILES):
-        allele_ref[:, t * LANES : (t + 1) * LANES] = p_now[t][:K]
+        allele_ref[:, t * LANES : (t + 1) * LANES] = tile_of(t)[:K]
+    wait_alleles_sent()
+
+
+def finish(mix_in, allele_in, mix_out, allele_out):
+    mix_out[...] = mix_in[...]
+    allele_out[...] = allele_in[...]
 
 
 def local(genotypes, observed, proportions, frequencies):
     vmem = pl.BlockSpec(memory_space=pltpu.VMEM)
     hbm = pl.BlockSpec(memory_space=pl.ANY)
     dma = pltpu.SemaphoreType.DMA
-    return pl.pallas_call(
+    outs = pl.pallas_call(
         kernel,
         name="em",
         out_shape=(
@@ -510,19 +524,17 @@
             pltpu.VMEM((SAMP, VARS), jnp.int32),
             pltpu.VMEM((SAMP, VARS), F32),
             pltpu.VMEM((SAMP, VARS), F32),
-            pltpu.VMEM((SAMP, LANES), F32),
-            pltpu.VMEM((SAMP, LANES), F32),
+            pltpu.VMEM((ROWS, SAMP), F32),
+            pltpu.VMEM((3 * ROWS, SAMP), F32),
             pltpu.VMEM((ROWS, SAMP), F32),
             pltpu.VMEM((ROWS, SAMP), F32),
-            pltpu.VMEM((ROWS, SAMP), F32),
-            pltpu.VMEM((TILES, ROWS, LANES), F32),
             pltpu.VMEM((TILES, ROWS, LANES), F32),
             pltpu.VMEM((TILES, ROWS, LANES), F32),
             pltpu.VMEM((SAMP, LANES), BF16),
             pltpu.VMEM((LANES, VARS), BF16),
             pltpu.VMEM((3 * ROWS, SAMP), BF16),
-            pltpu.VMEM((BLOCKS, 4 * CB, LANES), BF16),
-            pltpu.VMEM((2, RB, 4 * CB), BF16),
+            pltpu.VMEM((3 * ROWS, CB), BF16),
+            pltpu.VMEM((2, 4, RB, CB), BF16),
             pltpu.VMEM((K, SAMP), F32),
             pltpu.VMEM((K, 32), F32),
             pltpu.VMEM((8, LANES), F32),
@@ -537,7 +549,8 @@
             dma((2,)),
             dma((2,)),
             dma((2,)),
-            dma((2,)),
+            dma((1,)),
+            dma((BLOCKS,)),
             dma((1,)),
             dma((2,)),
             dma((2,)),
@@ -547,6 +560,16 @@
             collective_id=0, has_side_effects=True, vmem_limit_bytes=60 * 1024 * 1024
         ),
     )(genotypes, observed, proportions, frequencies)
+    return pl.pallas_call(
+        finish,
+        name="finish",
+        out_shape=(
+            jax.ShapeDtypeStruct((K, SAMP), F32),
+            jax.ShapeDtypeStruct((K, VARS), F32),
+        ),
+        in_specs=[vmem, vmem],
+        out_specs=(vmem, vmem),
+    )(*outs)
 
 
 def solution(mesh):

time: 115 us -> 104 us (0.904)
  Pallas kernels: 111 us -> 103 us
  local copies, waits for them, and re-layouts: 2.95 us -> 0 us
    pallas_call x1, Pallas kernels: 111 us -> 101 us  [local(): pl.pallas_call(kernel, name='em', out_shape=(jax.ShapeDtypeStruct((K, SAM...]
    unnamed x2 -> x0, local copies, waits for them, and re-layouts: 2.95 us -> none
    pallas_call x0 -> x1, Pallas kernels: none -> 1.53 us  [local(): pl.pallas_call(finish, name='finish', out_shape=(jax.ShapeDtypeStruct((K,...]
where the time goes in v3:
time: 104 us; the launch traced here: 103 us
  Pallas kernels  103 us (99%)
    pallas_call x1, Pallas kernels, local(): pl.pallas_call(kernel, name='em', out_shape=(jax.ShapeDtypeStruct((K, SAM...  101 us

profile of v3, /device:TPU:1, one launch (start us, length us, event | category | flops | bytes accessed | tf_op | source)
XLA Modules:
  0.0 103.4 jit_solution(17235651675237154599)
XLA Ops:
  0.6 101.2 %em.1 = (f32[10,1024]{1,0:T(8,128)}, f32[10,1024]{1,0:T(8,128)}) custom-call(s32[1024,1024]{1,0:T(8,128)} %geno_hbm.1, s32[1024,1024]{1,0:T(8,128)} %seen_hbm.1, f32[10,1024]{1,0:T(8,128)} %props_ref.1, f32[10,32]{1,0:T(8,128)} %freqs_ref.1), custom_call_target="tpu_custom_call" | custom-call | tf_op jit(solution)/shard_map/em/pallas_call | solution.py:513
  101.8 1.5 %finish.1 = (f32[10,1024]{1,0:T(8,128)}, f32[10,1024]{1,0:T(8,128)}) custom-call(f32[10,1024]{1,0:T(8,128)} %get-tuple-element.4.mix_in, f32[10,1024]{1,0:T(8,128)} %get-tuple-element.5.allele_in), custom_call_target="tpu_custom_call" | custom-call | tf_op jit(solution)/shard_map/finish/pallas_call | solution.py:563

commit v4 on v3

--- a/solution.py
+++ b/solution.py
@@ -18,7 +18,13 @@
 VARS = 1024
 LANES = 128
 TILES = VARS // LANES
-PIECES = 24
+HALF = K // 2
+PIECES = 2 * TILES
+SERVED = ((2, 0), (1, 1), (1, 3), (3, 0), (1, 0), (0, 3), (0, 1), (0, 0))
+SPREAD = sorted(
+    ((x, y, c) for x in range(4) for y in range(4) for c in range(2)),
+    key=lambda d: -(min(d[0], 4 - d[0]) + min(d[1], 4 - d[1])),
+)
 RB = 256
 CB = 256
 BLOCKS = VARS // CB
@@ -40,12 +46,6 @@
     mid = rest.astype(BF16).astype(F32)
     low = (rest - mid).astype(BF16).astype(F32)
     return high, mid, low
-
-
-def split2(values):
-    high = values.astype(BF16)
-    low = (values - high.astype(F32)).astype(BF16)
-    return high, low
 
 
 def dot(a, b):
@@ -89,9 +89,13 @@
     rs_send,
     rs_recv,
     ag_all,
-    z_all,
+    z_top,
+    z_rest,
+    c_all,
+    twice_ref,
     sq_q,
-    sq_p,
+    sp_all,
+    sp_out,
     load_sem,
     small_sem,
     f_sems,
@@ -100,15 +104,27 @@
     ag_recv,
     z_send,
     z_recv,
+    y_recv,
+    c_sems,
     sq_sems,
     sp_sems,
 ):
     s = lax.axis_index("samp")
     v = lax.axis_index("var")
-    my_piece = lax.rem(s, 2) * 16 + s // 2
-    is_owner = my_piece < PIECES
-    my_q = my_piece // TILES
-    my_t = lax.rem(my_piece, TILES)
+    chip_x = s // 8
+    chip_y = lax.rem(s // 2, 4)
+    core = lax.rem(s, 2)
+    my_t = lax.rem(chip_x, 2) * 4 + lax.rem(chip_y + 2 * (chip_x // 2), 4)
+    my_piece = core * TILES + my_t
+
+    along_x = [lax.rem(chip_x + d, 4) * 8 for d in range(4)]
+    along_y = [lax.rem(chip_y + d, 4) * 2 for d in range(4)]
+    cores = (core, 1 - core)
+    along_v = [lax.rem(v + d, NV) for d in range(NV)]
+
+    def moved(x, y, c):
+        return along_x[x] + along_y[y] + cores[c]
+
     home = s // TILES
 
     def remote(src, dst, send_sem, recv_sem, where):
@@ -186,16 +202,12 @@
 
     my_slot = NV * lax.rem(s, TILES) + v
 
-    def send_block(d, carry):
-        far_s = lax.rem(s + NS // 2 + d, NS)
-
-        @pl.when(jnp.logical_or(far_s != s, home != v))
-        def _():
-            remote(f_send, f_recv.at[my_slot], f_sems.at[0], f_sems.at[1], (far_s, home)).start()
-
-        return carry
-
-    lax.fori_loop(0, NS, send_block, 0)
+    for x, y, c in SPREAD:
+        copy = remote(f_send, f_recv.at[my_slot], f_sems.at[0], f_sems.at[1], (moved(x, y, c), home))
+        if (x, y, c) != (0, 0, 0):
+            copy.start()
+        else:
+            pl.when(home != v)(copy.start)
 
     small[1].wait()
     q_now[...] = jnp.concatenate([props_buf[...], jnp.zeros((ROWS - K, SAMP), F32)], axis=0)
@@ -208,8 +220,7 @@
 
     prep_q(q_now[...])
 
-    count_rows = lax.broadcasted_iota(jnp.int32, (ROWS, VARS), 0)
-    count_w = jnp.where(count_rows == K, 2.0, 0.0).astype(BF16)
+    count_w = jnp.full((ROWS, VARS), 2.0, BF16)
 
     def convert(chunk):
         for copy in load(chunk):
@@ -223,6 +234,11 @@
 
     for chunk in range(CHUNKS):
         convert(chunk)
+
+    c_all[v] = count_acc[:1, :]
+    c_slot = c_all.at[v]
+    for d in (2, 1, 3):
+        remote(c_slot, c_slot, c_sems.at[0], c_sems.at[1], (s, along_v[d])).start()
 
     @pl.when(home == v)
     def _():
@@ -245,6 +261,7 @@
                 rows8 = jnp.where(lane_group == m, got, rows8)
             halves.append(rows8)
         p_now[t] = jnp.concatenate(halves, axis=0)
+        p_start[t] = p_now[t]
 
     @pl.when(home == v)
     def _():
@@ -254,26 +271,24 @@
     def _():
         wait_bytes(f_recv, f_sems.at[0])
 
+    def pick(tile):
+        return jnp.where(core == 0, tile[:HALF], tile[HALF:K])
+
     def wait_alleles(cb):
-        mine = jnp.logical_and(is_owner, my_t // GROUP == cb)
-
-        @pl.when(mine)
+        @pl.when(my_t // GROUP == cb)
         def _():
-            wait_bytes(ag_all.at[pl.ds(0, 3 * GROUP - 1)], ag_recv.at[cb])
-
-        @pl.when(jnp.logical_not(mine))
+            wait_bytes(ag_all.at[pl.ds(0, 2 * GROUP - 1)], ag_recv.at[cb])
+
+        @pl.when(my_t // GROUP != cb)
         def _():
-            wait_bytes(ag_all.at[pl.ds(0, 3 * GROUP)], ag_recv.at[cb])
+            wait_bytes(ag_all.at[pl.ds(0, 2 * GROUP)], ag_recv.at[cb])
 
     def wait_alleles_sent():
-        @pl.when(is_owner)
-        def _():
-            wait_bytes(ag_all, ag_send.at[0])
-            wait_bytes(ag_all.at[pl.ds(0, NS - 1 - PIECES)], ag_send.at[0])
+        wait_bytes(ag_all.at[pl.ds(0, PIECES - 1)], ag_send.at[0])
 
     def tile_of(t):
         return jnp.concatenate(
-            [ag_all[t], ag_all[TILES + t], ag_all[2 * TILES + t], jnp.zeros((4, LANES), F32)],
+            [ag_all[t][:HALF], ag_all[TILES + t][:HALF], jnp.zeros((ROWS - K, LANES), F32)],
             axis=0,
         )
 
@@ -301,12 +316,13 @@
             cols = pl.ds(cb * CB, CB)
             rows = pl.ds(rb * RB, RB)
             expected = dot(q_cols[rows, :], p_rows[:, cols])
-            other = 1.0 - expected
-            inverse = 1.0 / (expected * other)
-            alt_high, alt_low = split2(alt_cnt[rows, cols] * (other * inverse))
-            ref_high, ref_low = split2(ref_cnt[rows, cols] * (expected * inverse))
-            for kind, part in enumerate((alt_high, alt_low, ref_high, ref_low)):
-                w_buf[slot, kind] = part
+            for side, (counts, chance) in enumerate(
+                ((alt_cnt, expected), (ref_cnt, 1.0 - expected))
+            ):
+                ratio = counts[rows, cols] * (1.0 / chance)
+                w_buf[slot, 2 * side] = ratio.astype(BF16)
+                high = w_buf[slot, 2 * side].astype(F32)
+                w_buf[slot, 2 * side + 1] = (ratio - high).astype(BF16)
 
         def stage_b(cb, rb, slot, sums):
             rows = pl.ds(rb * RB, RB)
@@ -326,81 +342,104 @@
             alt, ref = [a[:ROWS] + a[ROWS : 2 * ROWS] + a[2 * ROWS :] for a in sums]
             for t in range(cb * CB // LANES, (cb + 1) * CB // LANES):
                 lane = t * LANES - cb * CB
-                for part in range(3):
-                    piece = part * TILES + t
-                    target = (piece % 16) * 2 + piece // 16
-                    rs_send[piece] = jnp.concatenate(
-                        [
-                            alt[4 * part : 4 * part + 4, lane : lane + LANES],
-                            ref[4 * part : 4 * part + 4, lane : lane + LANES],
-                        ],
-                        axis=0,
-                    )
-
-                    @pl.when(s != target)
-                    def _():
-                        remote(
-                            rs_send.at[piece],
-                            rs_recv.at[s],
-                            rs_sems.at[0],
-                            rs_sems.at[1],
-                            (target, v),
-                        ).start()
+                for half in range(2):
+                    piece = half * TILES + t
+                    for row in range(HALF):
+                        k = half * HALF + row
+                        rs_send[piece, row] = jnp.concatenate(
+                            [a[k : k + 1, lane : lane + LANES] for a in (alt, ref)], axis=0
+                        )
+                    first = ((t // 4) * 4 + t % 4) * 2 + half
+                    other = ((t // 4 + 2) * 4 + (t + 2) % 4) * 2 + half
+                    for target in (first, other):
+
+                        @pl.when(s != target)
+                        def _():
+                            remote(
+                                rs_send.at[piece],
+                                rs_recv.at[parity, s],
+                                rs_sems.at[2],
+                                rs_sems.at[parity],
+                                (target, v),
+                            ).start()
 
         for cb in range(BLOCKS):
             prep_p(cb)
             sums = None
             stage_a(cb, 0, 0)
+            stage_a(cb, 1, 1)
             for rb in range(SAMP // RB):
-                if rb + 1 < SAMP // RB:
-                    stage_a(cb, rb + 1, (rb + 1) % 2)
-                sums = stage_b(cb, rb, rb % 2, sums)
+                if rb + 2 < SAMP // RB:
+                    stage_a(cb, rb + 2, (rb + 2) % 4)
+                sums = stage_b(cb, rb, rb % 4, sums)
             send_pieces(cb, sums)
 
-        z_all[parity, v] = count_acc[...] + (
-            prop_acc[:ROWS, :] + prop_acc[ROWS : 2 * ROWS, :] + prop_acc[2 * ROWS :, :]
-        )
-
-        def send_z(d, carry):
-            slot = z_all.at[parity, v]
-            remote(slot, slot, z_send.at[0], z_recv.at[parity], (s, lax.rem(v + d, NV))).start()
-            return carry
-
-        lax.fori_loop(1, NV, send_z, 0)
-
-        @pl.when(is_owner)
-        def _():
-            wait_bytes(rs_recv.at[pl.ds(0, NS - 1)], rs_sems.at[1])
-            rs_recv[s] = rs_send[my_piece]
-            sums = [rs_recv[i] for i in range(NS)]
+        prop = prop_acc[:ROWS, :] + prop_acc[ROWS : 2 * ROWS, :] + prop_acc[2 * ROWS :, :]
+        z_top[parity, v] = prop[:8]
+        z_rest[parity, v] = prop[8:K]
+        top_slot = z_top.at[parity, v]
+        rest_slot = z_rest.at[parity, v]
+        for d in (2, 1, 3):
+            where = (s, along_v[d])
+            remote(top_slot, top_slot, z_send.at[0], z_recv.at[parity], where).start()
+            remote(rest_slot, rest_slot, z_send.at[1], y_recv.at[parity], where).start()
+
+        def own_piece():
+            wait_bytes(rs_recv.at[parity, pl.ds(0, NS - 1)], rs_sems.at[parity])
+            rs_recv[parity, s] = rs_send[my_piece]
+            sums = [rs_recv[parity, i] for i in range(NS)]
             while len(sums) > 1:
                 sums = [sums[i] + sums[i + 1] for i in range(0, len(sums), 2)]
-            alt_sum, ref_sum = sums[0][:4], sums[0][4:]
-            tile = p_now[my_t]
-            old = jnp.where(my_q == 0, tile[:4], jnp.where(my_q == 1, tile[4:8], tile[8:12]))
+            alt_sum, ref_sum = sums[0][:, 0, :], sums[0][:, 1, :]
+            old = pick(p_now[my_t])
             weighted = old * alt_sum
             new = clip_unit(weighted / (weighted + (1.0 - old) * ref_sum))
-            piece_row = 4 * my_q + lax.broadcasted_iota(jnp.int32, (4, LANES), 0)
 
             @pl.when(step > 0)
             def _():
                 wait_alleles_sent()
 
-            ag_all[my_piece] = jnp.where(piece_row < K, new, 0.0)
-
-            def send_ag(d, carry):
-                slot = ag_all.at[my_piece]
-                remote(
-                    slot, slot, ag_send.at[0], ag_recv.at[my_t // GROUP], (lax.rem(s + d, NS), v)
-                ).start()
-                return carry
-
-            lax.fori_loop(1, NS, send_ag, 0)
-
-        wait_bytes(z_all.at[parity, pl.ds(0, NV - 1)], z_recv.at[parity])
+            r = old - pick(p_start[my_t])
+            c = new - old - r
+            squares = [jnp.sum(x * x, axis=0, keepdims=True) for x in (r, c)]
+            squares = jnp.concatenate(squares, axis=0)
+            ag_all[my_piece] = jnp.concatenate([new, squares, jnp.zeros((1, LANES), F32)], axis=0)
+            ag_slot = ag_all.at[my_piece]
+            for x, y in SERVED:
+                for c in range(2):
+                    if (x, y, c) != (0, 0, 0):
+                        remote(
+                            ag_slot, ag_slot, ag_send.at[0], ag_recv.at[my_t // GROUP], (moved(x, y, c), v)
+                        ).start()
+
+            @pl.when(phase == 1)
+            def _():
+                sp_out[...] = squares
+                for d in (2, 1, 3):
+                    for x, y in SERVED:
+                        for c in range(2):
+                            remote(
+                                sp_out, sp_all.at[v, my_piece], sp_sems.at[0], sp_sems.at[1], (moved(x, y, c), along_v[d])
+                            ).start()
+
+        last_block = my_t // GROUP == BLOCKS - 1
+        relaxed = jnp.logical_and(phase != 1, step < 3 * STEPS - 1)
+        late = jnp.logical_and(last_block, relaxed)
+        pl.when(jnp.logical_not(late))(own_piece)
+
+        @pl.when(step == 0)
+        def _():
+            wait_bytes(c_all.at[pl.ds(0, NV - 1)], c_sems.at[1])
+            twice_ref[...] = c_all[0] + c_all[1] + c_all[2] + c_all[3]
+            wait_bytes(c_all.at[pl.ds(0, NV - 1)], c_sems.at[0])
+
+        wait_bytes(z_top.at[parity, pl.ds(0, NV - 1)], z_recv.at[parity])
+        wait_bytes(z_rest.at[parity, pl.ds(0, NV - 1)], y_recv.at[parity])
         q = q_now[...]
-        total = z_all[parity, 0] + z_all[parity, 1] + z_all[parity, 2] + z_all[parity, 3]
-        twice = total[K : K + 1, :]
+        top = z_top[parity, 0] + z_top[parity, 1] + z_top[parity, 2] + z_top[parity, 3]
+        rest = z_rest[parity, 0] + z_rest[parity, 1] + z_rest[parity, 2] + z_rest[parity, 3]
+        total = jnp.concatenate([top, rest, jnp.zeros((ROWS - K, SAMP), F32)], axis=0)
+        twice = twice_ref[...]
         inner = jnp.sum(q * total, axis=0, keepdims=True)
         q_next = jnp.where(row_mask, clip_unit(q * (1.0 + (total - inner) / twice)), 0.0)
 
@@ -415,12 +454,12 @@
                 part = part + row[:, t * LANES : (t + 1) * LANES]
             sq_q[s] = part
 
-            def send_sq(d, carry):
-                slot = sq_q.at[s]
-                remote(slot, slot, sq_sems.at[0], sq_sems.at[1], (lax.rem(s + d, NS), v)).start()
-                return carry
-
-            lax.fori_loop(1, NS, send_sq, 0)
+            sq_slot = sq_q.at[s]
+            for x, y, c in SPREAD:
+                if (x, y, c) != (0, 0, 0):
+                    remote(
+                        sq_slot, sq_slot, sq_sems.at[0], sq_sems.at[1], (moved(x, y, c), v)
+                    ).start()
 
         @pl.when(phase != 1)
         def _():
@@ -428,30 +467,13 @@
             q_now[...] = q_next
             prep_q(q_next)
 
+        pl.when(late)(own_piece)
+
         @pl.when(phase == 1)
         def _():
             for cb in range(BLOCKS):
                 wait_alleles(cb)
             p_next = [tile_of(t) for t in range(TILES)]
-            part_r = jnp.zeros((ROWS, LANES), F32)
-            part_v = jnp.zeros((ROWS, LANES), F32)
-            for t in range(TILES):
-                r = p_now[t] - p_start[t]
-                c = p_next[t] - p_now[t] - r
-                part_r = part_r + r * r
-                part_v = part_v + c * c
-            sq_p[v] = jnp.concatenate(
-                [jnp.sum(part_r, axis=0, keepdims=True), jnp.sum(part_v, axis=0, keepdims=True)],
-                axis=0,
-            )
-
-            def send_sp(d, carry):
-                slot = sq_p.at[v]
-                remote(slot, slot, sp_sems.at[0], sp_sems.at[1], (s, lax.rem(v + d, NV))).start()
-                return carry
-
-            lax.fori_loop(1, NV, send_sp, 0)
-
             def alpha_of(sums):
                 first = jnp.sum(sums[0:1], axis=1, keepdims=True)
                 second = jnp.sum(sums[1:2], axis=1, keepdims=True)
@@ -471,8 +493,11 @@
             q_now[...] = extra
             prep_q(extra)
 
-            wait_bytes(sq_p.at[pl.ds(0, NV - 1)], sp_sems.at[1])
-            alpha_p = alpha_of(sq_p[0] + sq_p[1] + sq_p[2] + sq_p[3])
+            for piece in range(PIECES):
+                sp_all[v, piece] = ag_all[piece][HALF : HALF + 2]
+            wait_bytes(sp_all.at[pl.ds(0, NV - 1)], sp_sems.at[1])
+            sums = [jnp.sum(sp_all[i], axis=0) for i in range(NV)]
+            alpha_p = alpha_of((sums[0] + sums[1]) + (sums[2] + sums[3]))
             for t in range(TILES):
                 base_p = p_start[t]
                 r = p_now[t] - base_p
@@ -481,15 +506,12 @@
                 p_now[t] = jnp.where(row_mask, extra_p, 0.0)
 
             wait_bytes(sq_q.at[pl.ds(0, NS - 1)], sq_sems.at[0])
-            wait_bytes(sq_p.at[pl.ds(0, NV - 1)], sp_sems.at[0])
-
-        wait_bytes(z_all.at[parity, pl.ds(0, NV - 1)], z_send.at[0])
-        wait_bytes(rs_send.at[pl.ds(0, PIECES - 1)], rs_sems.at[0])
-
-        @pl.when(jnp.logical_not(is_owner))
-        def _():
-            wait_bytes(rs_send.at[0], rs_sems.at[0])
-
+            wait_bytes(sp_all.at[pl.ds(0, NV - 1)], sp_sems.at[0])
+
+        wait_bytes(z_top.at[parity, pl.ds(0, NV - 1)], z_send.at[0])
+        wait_bytes(z_rest.at[parity, pl.ds(0, NV - 1)], z_send.at[1])
+        wait_bytes(rs_send, rs_sems.at[2])
+        wait_bytes(rs_send.at[pl.ds(0, PIECES - 1)], rs_sems.at[2])
         return carry
 
     lax.fori_loop(0, 3 * STEPS, em_step, 0)
@@ -534,24 +556,30 @@
             pltpu.VMEM((LANES, VARS), BF16),
             pltpu.VMEM((3 * ROWS, SAMP), BF16),
             pltpu.VMEM((3 * ROWS, CB), BF16),
-            pltpu.VMEM((2, 4, RB, CB), BF16),
+            pltpu.VMEM((4, 4, RB, CB), BF16),
             pltpu.VMEM((K, SAMP), F32),
             pltpu.VMEM((K, 32), F32),
             pltpu.VMEM((8, LANES), F32),
             pltpu.VMEM((NS, 8, LANES), F32),
+            pltpu.VMEM((PIECES, HALF, 2, LANES), F32),
+            pltpu.VMEM((2, NS, HALF, 2, LANES), F32),
             pltpu.VMEM((PIECES, 8, LANES), F32),
-            pltpu.VMEM((NS, 8, LANES), F32),
-            pltpu.VMEM((PIECES, 4, LANES), F32),
-            pltpu.VMEM((2, NV, ROWS, SAMP), F32),
+            pltpu.VMEM((2, NV, 8, SAMP), F32),
+            pltpu.VMEM((2, NV, K - 8, SAMP), F32),
+            pltpu.VMEM((NV, 1, SAMP), F32),
+            pltpu.VMEM((1, SAMP), F32),
             pltpu.VMEM((NS, 2, LANES), F32),
-            pltpu.VMEM((NV, 2, LANES), F32),
+            pltpu.VMEM((NV, PIECES, 2, LANES), F32),
+            pltpu.VMEM((2, LANES), F32),
             dma((2, CHUNKS)),
             dma((2,)),
             dma((2,)),
-            dma((2,)),
+            dma((3,)),
             dma((1,)),
             dma((BLOCKS,)),
-            dma((1,)),
+            dma((2,)),
+            dma((2,)),
+            dma((2,)),
             dma((2,)),
             dma((2,)),
             dma((2,)),

time: 104 us -> 94.6 us (0.910)
  Pallas kernels: 103 us -> 93.8 us
    pallas_call x1, Pallas kernels: 101 us -> 92.3 us  [local(): pl.pallas_call(kernel, name='em', out_shape=(jax.ShapeDtypeStruct((K, SAM...]
where the time goes in v4:
time: 94.6 us; the launch traced here: 94.4 us
  Pallas kernels  93.8 us (99%)
    pallas_call x1, Pallas kernels, local(): pl.pallas_call(kernel, name='em', out_shape=(jax.ShapeDtypeStruct((K, SAM...  92.3 us

profile of v4, /device:TPU:1, one launch (start us, length us, event | category | flops | bytes accessed | tf_op | source)
XLA Modules:
  0.0 94.4 jit_solution(2195731335535969929)
XLA Ops:
  0.6 92.3 %em.1 = (f32[10,1024]{1,0:T(8,128)}, f32[10,1024]{1,0:T(8,128)}) custom-call(s32[1024,1024]{1,0:T(8,128)} %geno_hbm.1, s32[1024,1024]{1,0:T(8,128)} %seen_hbm.1, f32[10,1024]{1,0:T(8,128)} %props_ref.1, f32[10,32]{1,0:T(8,128)} %freqs_ref.1), custom_call_target="tpu_custom_call" | custom-call | tf_op jit(solution)/shard_map/em/pallas_call | solution.py:535
  92.9 1.5 %finish.1 = (f32[10,1024]{1,0:T(8,128)}, f32[10,1024]{1,0:T(8,128)}) custom-call(f32[10,1024]{1,0:T(8,128)} %get-tuple-element.4.mix_in, f32[10,1024]{1,0:T(8,128)} %get-tuple-element.5.allele_in), custom_call_target="tpu_custom_call" | custom-call | tf_op jit(solution)/shard_map/finish/pallas_call | solution.py:591

commit v5 on v4

--- a/solution.py
+++ b/solution.py
@@ -316,10 +316,13 @@
             cols = pl.ds(cb * CB, CB)
             rows = pl.ds(rb * RB, RB)
             expected = dot(q_cols[rows, :], p_rows[:, cols])
+            ratios = []
             for side, (counts, chance) in enumerate(
                 ((alt_cnt, expected), (ref_cnt, 1.0 - expected))
             ):
-                ratio = counts[rows, cols] * (1.0 / chance)
+                ratios.append(counts[rows, cols] * (1.0 / chance))
+            ratios.append(ratios[0] - ratios[1])
+            for side, ratio in enumerate(ratios):
                 w_buf[slot, 2 * side] = ratio.astype(BF16)
                 high = w_buf[slot, 2 * side].astype(F32)
                 w_buf[slot, 2 * side + 1] = (ratio - high).astype(BF16)
@@ -329,12 +332,10 @@
             q_part = q_rows[:, rows]
             p_part = p_three[...]
             sides = []
-            props = []
             for side in range(2):
                 high, low = w_buf[slot, 2 * side], w_buf[slot, 2 * side + 1]
                 sides.append(dot(q_part, high) + dot(q_part, low))
-                props.append(dot_t(p_part, high) + dot_t(p_part, low))
-            prop = props[0] - props[1]
+            prop = dot_t(p_part, w_buf[slot, 4]) + dot_t(p_part, w_buf[slot, 5])
             prop_acc[:, rows] = prop if cb == 0 else prop_acc[:, rows] + prop
             return sides if sums is None else [sums[i] + sides[i] for i in range(2)]
 
@@ -556,7 +557,7 @@
             pltpu.VMEM((LANES, VARS), BF16),
             pltpu.VMEM((3 * ROWS, SAMP), BF16),
             pltpu.VMEM((3 * ROWS, CB), BF16),
-            pltpu.VMEM((4, 4, RB, CB), BF16),
+            pltpu.VMEM((4, 6, RB, CB), BF16),
             pltpu.VMEM((K, SAMP), F32),
             pltpu.VMEM((K, 32), F32),
             pltpu.VMEM((8, LANES), F32),

time: 94.6 us -> 91.4 us (0.966)
  Pallas kernels: 93.8 us -> 90.6 us
    pallas_call x1, Pallas kernels: 92.3 us -> 89.1 us  [local(): pl.pallas_call(kernel, name='em', out_shape=(jax.ShapeDtypeStruct((K, SAM...]
where the time goes in v5:
time: 91.4 us; the launch traced here: 91.2 us
  Pallas kernels  90.6 us (99%)
    pallas_call x1, Pallas kernels, local(): pl.pallas_call(kernel, name='em', out_shape=(jax.ShapeDtypeStruct((K, SAM...  89.1 us

profile of v5, /device:TPU:1, one launch (start us, length us, event | category | flops | bytes accessed | tf_op | source)
XLA Modules:
  0.0 91.2 jit_solution(7836023047947162552)
XLA Ops:
  0.6 89.1 %em.1 = (f32[10,1024]{1,0:T(8,128)}, f32[10,1024]{1,0:T(8,128)}) custom-call(s32[1024,1024]{1,0:T(8,128)} %geno_hbm.1, s32[1024,1024]{1,0:T(8,128)} %seen_hbm.1, f32[10,1024]{1,0:T(8,128)} %props_ref.1, f32[10,32]{1,0:T(8,128)} %freqs_ref.1), custom_call_target="tpu_custom_call" | custom-call | tf_op jit(solution)/shard_map/em/pallas_call | solution.py:536
  89.7 1.5 %finish.1 = (f32[10,1024]{1,0:T(8,128)}, f32[10,1024]{1,0:T(8,128)}) custom-call(f32[10,1024]{1,0:T(8,128)} %get-tuple-element.4.mix_in, f32[10,1024]{1,0:T(8,128)} %get-tuple-element.5.allele_in), custom_call_target="tpu_custom_call" | custom-call | tf_op jit(solution)/shard_map/finish/pallas_call | solution.py:592

commit v6 on v5

--- a/solution.py
+++ b/solution.py
@@ -34,6 +34,10 @@
 
 F32 = jnp.float32
 BF16 = jnp.bfloat16
+FAR = sorted(
+    ((x, y, c, d) for x, y in SERVED for c in range(2) for d in range(1, NV)),
+    key=lambda e: -sum(min(a, 4 - a) for a in (e[0], e[1], e[3])),
+)
 
 
 def clip_unit(values):
@@ -147,6 +151,25 @@
             pltpu.make_async_copy(seen_hbm.at[rows], seen_buf.at[rows], load_sem.at[1, chunk]),
         )
 
+    barrier = pltpu.get_barrier_semaphore()
+
+    def greet(where):
+        pl.semaphore_signal(barrier, inc=1, device_id=where, device_id_type=MESH)
+
+    first_source = v * TILES
+    for i in range(NS):
+        source = (first_source + i // NV, i % NV)
+
+        @pl.when(jnp.logical_or(source[0] != s, v != source[1]))
+        def _():
+            greet(source)
+
+    for x, y, c in SPREAD:
+        if (x, y, c) != (0, 0, 0):
+            greet((moved(x, y, c), v))
+    for d in (2, 1, 3):
+        greet((s, along_v[d]))
+
     small = (
         pltpu.make_async_copy(freqs_ref, freqs_buf, small_sem.at[0]),
         pltpu.make_async_copy(props_ref, props_buf, small_sem.at[1]),
@@ -157,40 +180,13 @@
         for copy in load(chunk):
             copy.start()
 
-    barrier = pltpu.get_barrier_semaphore()
-
-    def greet(where):
-        pl.semaphore_signal(barrier, inc=1, device_id=where, device_id_type=MESH)
-
-    def greet_samp(d, carry):
-        greet((lax.rem(s + d, NS), v))
-        return carry
-
-    def greet_var(d, carry):
-        greet((s, lax.rem(v + d, NV)))
-        return carry
-
-    def greet_source(i, carry):
-        far_s = v * TILES + i // NV
-        far_v = lax.rem(i, NV)
-
-        @pl.when(jnp.logical_or(far_s != s, far_v != v))
-        def _():
-            greet((far_s, far_v))
-
-        return carry
-
-    lax.fori_loop(0, NS, greet_source, 0)
-    lax.fori_loop(1, NV, greet_var, 0)
-    lax.fori_loop(1, NS, greet_samp, 0)
-
     row_ids = lax.broadcasted_iota(jnp.int32, (ROWS, 1), 0)
     row_mask = row_ids < K
 
     small[0].wait()
     block = freqs_buf[...]
-    tail = jnp.concatenate([block[8:K], jnp.zeros((ROWS - K, 32), F32)], axis=0)
-    f_send[...] = jnp.concatenate([block[:8], tail, jnp.zeros((8, 64), F32)], axis=1)
+    tail = jnp.concatenate([block[8:K], jnp.zeros((12 - K, 32), F32)], axis=0)
+    f_send[...] = jnp.concatenate([block[:4], block[4:8], tail, jnp.zeros((4, 32), F32)], axis=1)
 
     @pl.when(home == v)
     def _():
@@ -249,18 +245,18 @@
     def _():
         wait_bytes(f_recv, f_sems.at[1])
 
-    lane_group = lax.broadcasted_iota(jnp.int32, (8, LANES), 1) // 32
+    lane_group = lax.broadcasted_iota(jnp.int32, (4, LANES), 1) // 32
     for t in range(TILES):
-        halves = []
-        for half in range(2):
-            rows8 = jnp.zeros((8, LANES), F32)
+        groups = []
+        for group in range(3):
+            rows4 = jnp.zeros((4, LANES), F32)
             for m in range(NV):
-                shift = (32 * (m - half)) % LANES
+                shift = (32 * (m - group)) % LANES
                 got = f_recv[NV * t + m]
                 got = pltpu.roll(got, shift, 1) if shift else got
-                rows8 = jnp.where(lane_group == m, got, rows8)
-            halves.append(rows8)
-        p_now[t] = jnp.concatenate(halves, axis=0)
+                rows4 = jnp.where(lane_group == m, got, rows4)
+            groups.append(rows4)
+        p_now[t] = jnp.concatenate(groups + [jnp.zeros((4, LANES), F32)], axis=0)
         p_start[t] = p_now[t]
 
     @pl.when(home == v)
@@ -416,12 +412,10 @@
             @pl.when(phase == 1)
             def _():
                 sp_out[...] = squares
-                for d in (2, 1, 3):
-                    for x, y in SERVED:
-                        for c in range(2):
-                            remote(
-                                sp_out, sp_all.at[v, my_piece], sp_sems.at[0], sp_sems.at[1], (moved(x, y, c), along_v[d])
-                            ).start()
+                for x, y, c, d in FAR:
+                    remote(
+                        sp_out, sp_all.at[v, my_piece], sp_sems.at[0], sp_sems.at[1], (moved(x, y, c), along_v[d])
+                    ).start()
 
         last_block = my_t // GROUP == BLOCKS - 1
         relaxed = jnp.logical_and(phase != 1, step < 3 * STEPS - 1)
@@ -560,8 +554,8 @@
             pltpu.VMEM((4, 6, RB, CB), BF16),
             pltpu.VMEM((K, SAMP), F32),
             pltpu.VMEM((K, 32), F32),
-            pltpu.VMEM((8, LANES), F32),
-            pltpu.VMEM((NS, 8, LANES), F32),
+            pltpu.VMEM((4, LANES), F32),
+            pltpu.VMEM((NS, 4, LANES), F32),
             pltpu.VMEM((PIECES, HALF, 2, LANES), F32),
             pltpu.VMEM((2, NS, HALF, 2, LANES), F32),
             pltpu.VMEM((PIECES, 8, LANES), F32),

time: 91.4 us -> 90.8 us (level)
  no operation moved by 1% of the time
where the time goes in v6:
time: 90.8 us; the launch traced here: 90.7 us
  Pallas kernels  90.1 us (99%)
    pallas_call x1, Pallas kernels, local(): pl.pallas_call(kernel, name='em', out_shape=(jax.ShapeDtypeStruct((K, SAM...  88.5 us

profile of v6, /device:TPU:1, one launch (start us, length us, event | category | flops | bytes accessed | tf_op | source)
XLA Modules:
  0.0 90.7 jit_solution(18026187823532660744)
XLA Ops:
  0.6 88.5 %em.1 = (f32[10,1024]{1,0:T(8,128)}, f32[10,1024]{1,0:T(8,128)}) custom-call(s32[1024,1024]{1,0:T(8,128)} %geno_hbm.1, s32[1024,1024]{1,0:T(8,128)} %seen_hbm.1, f32[10,1024]{1,0:T(8,128)} %props_ref.1, f32[10,32]{1,0:T(8,128)} %freqs_ref.1), custom_call_target="tpu_custom_call" | custom-call | tf_op jit(solution)/shard_map/em/pallas_call | solution.py:530
  89.2 1.5 %finish.1 = (f32[10,1024]{1,0:T(8,128)}, f32[10,1024]{1,0:T(8,128)}) custom-call(f32[10,1024]{1,0:T(8,128)} %get-tuple-element.4.mix_in, f32[10,1024]{1,0:T(8,128)} %get-tuple-element.5.allele_in), custom_call_target="tpu_custom_call" | custom-call | tf_op jit(solution)/shard_map/finish/pallas_call | solution.py:586

commit v7 on v6

--- a/solution.py
+++ b/solution.py
@@ -210,8 +210,7 @@
 
     def prep_q(q):
         qh, qm, ql = split3(q)
-        pad = jnp.zeros((2 * ROWS, SAMP), F32)
-        q_cols[...] = jnp.concatenate([qh, qh, qm, qm, qh, ql, pad], axis=0).T.astype(BF16)
+        q_cols[...] = jnp.concatenate([qh, qh, qm, qm, qh, ql], axis=0).T.astype(BF16)
         q_rows[...] = jnp.concatenate([qh, qm, ql], axis=0).astype(BF16)
 
     prep_q(q_now[...])
@@ -303,9 +302,8 @@
 
             p = jnp.concatenate([p_now[t] for t in range(cb * GROUP, (cb + 1) * GROUP)], axis=1)
             ph, pm, pL = split3(p)
-            pad = jnp.zeros((2 * ROWS, CB), F32)
             cols = pl.ds(cb * CB, CB)
-            p_rows[:, cols] = jnp.concatenate([ph, pm, ph, pm, pL, ph, pad], axis=0).astype(BF16)
+            p_rows[:, cols] = jnp.concatenate([ph, pm, ph, pm, pL, ph], axis=0).astype(BF16)
             p_three[...] = jnp.concatenate([ph, pm, pL], axis=0).astype(BF16)
 
         def stage_a(cb, rb, slot):
@@ -547,8 +545,8 @@
             pltpu.VMEM((ROWS, SAMP), F32),
             pltpu.VMEM((TILES, ROWS, LANES), F32),
             pltpu.VMEM((TILES, ROWS, LANES), F32),
-            pltpu.VMEM((SAMP, LANES), BF16),
-            pltpu.VMEM((LANES, VARS), BF16),
+            pltpu.VMEM((SAMP, 6 * ROWS), BF16),
+            pltpu.VMEM((6 * ROWS, VARS), BF16),
             pltpu.VMEM((3 * ROWS, SAMP), BF16),
             pltpu.VMEM((3 * ROWS, CB), BF16),
             pltpu.VMEM((4, 6, RB, CB), BF16),

time: 90.8 us -> 91.1 us (level)
  no operation moved by 1% of the time
where the time goes in v7:
time: 91.1 us; the launch traced here: 90.9 us
  Pallas kernels  90.3 us (99%)
    pallas_call x1, Pallas kernels, local(): pl.pallas_call(kernel, name='em', out_shape=(jax.ShapeDtypeStruct((K, SAM...  88.8 us

profile of v7, /device:TPU:1, one launch (start us, length us, event | category | flops | bytes accessed | tf_op | source)
XLA Modules:
  0.0 90.9 jit_solution(9672317109763428082)
XLA Ops:
  0.6 88.8 %em.1 = (f32[10,1024]{1,0:T(8,128)}, f32[10,1024]{1,0:T(8,128)}) custom-call(s32[1024,1024]{1,0:T(8,128)} %geno_hbm.1, s32[1024,1024]{1,0:T(8,128)} %seen_hbm.1, f32[10,1024]{1,0:T(8,128)} %props_ref.1, f32[10,32]{1,0:T(8,128)} %freqs_ref.1), custom_call_target="tpu_custom_call" | custom-call | tf_op jit(solution)/shard_map/em/pallas_call | solution.py:528
  89.4 1.5 %finish.1 = (f32[10,1024]{1,0:T(8,128)}, f32[10,1024]{1,0:T(8,128)}) custom-call(f32[10,1024]{1,0:T(8,128)} %get-tuple-element.4.mix_in, f32[10,1024]{1,0:T(8,128)} %get-tuple-element.5.allele_in), custom_call_target="tpu_custom_call" | custom-call | tf_op jit(solution)/shard_map/finish/pallas_call | solution.py:584
